TPU v7x, 256 devices: a whole 4x4x8 slice. The times are simulated.
256 devices in a mesh: beam: 16 (over x, z_hi, core), depth: 16 (over y, z_lo).
Axes of the slice: x: 4, y: 4, z: 8 (z_hi: 2, z_lo: 4; z = z_hi * 4 + z_lo), core: 2. Of those that a mesh axis runs over, the one named last changes fastest.
Arguments:
- concentration: float32 [512, 2048, 256], P('beam', 'depth'), may hold values from 0.25 to 2.5
- entry_intensity: float32 [2048, 256], P('depth'), may hold values from 0.25 to 1.75
- absorb: float32 [256], replicated, may hold values from 0.000390625 to 0.0048828125
- blur_taps: float32 [5], replicated, may hold values from 0.1 to 1
- measured: float32 [512, 256], P('beam'), may hold values from -6 to 6
Outputs:
- descent: float32 [512, 2048, 256], P('beam', 'depth')
- residual: float32 [512, 256], P('beam', 'depth')
All inputs are finite; a program needn't handle non-finite values.
Results may differ from a plain program's by a relative error of at most 0.000058.
Values sent between devices are 32-bit elements; how exact they have to be, the bound alone decides.
No kernel may reach another device: no remote copies, remote signals or barrier semaphores. Data moves between devices by JAX's collectives and lax.ppermute only.
A program may use at most 64 MiB of HBM per device.

v0:
```python
import jax
import jax.numpy as jnp
from jax import lax
from jax.experimental import pallas as pl
from jax.experimental.pallas import tpu as pltpu
from jax.sharding import Mesh
from jax.sharding import PartitionSpec as P

BEAM = ("x", "zh", "core")
DEPTH = ("y", "zl")
LOG2E = 1.4426950408889634
CHUNKS = 8
VM = pl.BlockSpec(memory_space=pltpu.VMEM)
SM = pl.BlockSpec(memory_space=pltpu.SMEM)
HBM = pl.BlockSpec(memory_space=pltpu.HBM)
F32 = jnp.float32


def xor(count, bits):
    return [(i, i ^ bits) for i in range(count)]


def call(body, outs, in_specs, out_specs, flops, nbytes, exps=0, scratch=()):
    return pl.pallas_call(
        body,
        out_shape=outs,
        in_specs=in_specs,
        out_specs=out_specs,
        scratch_shapes=scratch,
        cost_estimate=pl.CostEstimate(flops=flops, bytes_accessed=nbytes, transcendentals=exps),
        compiler_params=pltpu.CompilerParams(vmem_limit_bytes=8 * 2**20),
    )


def halves(ref, total):
    rows = total.shape[0] // 2
    core = lax.axis_index("core")
    ref[...] = total
    mine = ref[pl.ds(pl.multiple_of(core * rows, 8), rows), :]
    other = ref[pl.ds(pl.multiple_of((1 - core) * rows, 8), rows), :]
    return mine, other


def joined(ref, mine, other):
    rows = mine.shape[0]
    core = lax.axis_index("core")
    ref[pl.ds(pl.multiple_of(core * rows, 8), rows), :] = mine
    ref[pl.ds(pl.multiple_of((1 - core) * rows, 8), rows), :] = other
    return ref[...]


def load_body(c_hbm, c_ref, mine_ref, other_ref, flag_ref, total_ref, sems):
    beam = c_ref.shape[0]
    step = beam // CHUNKS
    copies = []
    for k in range(CHUNKS):
        part = pl.ds(k * step, step)
        copy = pltpu.make_async_copy(c_hbm.at[part], c_ref.at[part], sems.at[k])
        copy.start()
        copies.append(copy)
    x, zh, core = (lax.axis_index(name) for name in BEAM)
    flags = [zh, core] + [((x ^ k) < x).astype(jnp.int32) for k in (1, 2, 3)]
    for k, flag in enumerate(flags):
        flag_ref[k : k + 1, :] = jnp.full((1, flag_ref.shape[1]), flag.astype(F32))
    total = None
    for k in range(CHUNKS):
        copies[k].wait()
        part = jnp.sum(c_ref[k * step : (k + 1) * step], axis=0)
        total = part if total is None else total + part
    mine_ref[...], other_ref[...] = halves(total_ref, total)


def local_body(c_ref, absorb_ref, light_ref, emit_ref):
    beam, depth, height = c_ref.shape
    rate = jnp.broadcast_to(absorb_ref[...] * (-LOG2E), (8, height))

    @pl.loop(0, depth // 8)
    def _(i):
        rows = pl.ds(pl.multiple_of(i * 8, 8), 8)
        prior = jnp.zeros((8, height), F32)
        for b in range(beam):
            c = c_ref[b, rows, :]
            light = jnp.exp2(rate * prior)
            light_ref[b, rows, :] = light
            emit_ref[b, rows, :] = light * c
            prior = prior + c


def image_body(mine_ref, other_ref, absorb_ref, entry_ref, emit_ref, entered_ref, part_ref, before_ref):
    beam = emit_ref.shape[0]
    before = joined(before_ref, mine_ref[...], other_ref[...])
    entered = entry_ref[...] * jnp.exp2(before * (absorb_ref[...] * (-LOG2E)))
    entered_ref[...] = entered
    for b in range(beam):
        part_ref[b : b + 1, :] = jnp.sum(entered * emit_ref[b], axis=0, keepdims=True)


def shifted(value, by):
    width = value.shape[1]
    column = lax.broadcasted_iota(jnp.int32, value.shape, 1)
    source = column + by
    moved = pltpu.roll(value, (-by) % width, 1)
    return jnp.where((source >= 0) & (source < width), moved, 0.0)


def blurred(value, taps_ref, sign):
    total = taps_ref[2] * value
    for k in (0, 1, 3, 4):
        total = total + taps_ref[k] * shifted(value, sign * (k - 2))
    return total


def adjoint_body(scale, s0, s1, s2, s3, taps_ref, measured_ref, emit_ref, entered_ref,
                 residual_ref, back_ref, mine_ref, other_ref, total_ref):
    beam = emit_ref.shape[0]
    image = (s0[...] + s1[...] + s2[...] + s3[...]) * scale
    residual = blurred(image, taps_ref, 1) - measured_ref[...]
    residual_ref[...] = residual
    back_ref[...] = blurred(residual, taps_ref, -1)
    total = None
    for b in range(beam):
        term = back_ref[b : b + 1, :] * emit_ref[b]
        total = term if total is None else total + term
    mine_ref[...], other_ref[...] = halves(total_ref, total * entered_ref[...])


def partial_body(absorb_ref, back_ref, residual_ref, entered_ref, light_ref, emit_ref,
                 known_ref, columns_ref, turned_ref):
    beam, depth, height = light_ref.shape
    width = columns_ref.shape[0]
    section = (lax.axis_index("y") * lax.axis_size("zl") + lax.axis_index("zl")) * width
    turned_ref[...] = residual_ref[...].T
    columns_ref[...] = turned_ref[pl.ds(pl.multiple_of(section, 8), width), :]
    absorb = jnp.broadcast_to(absorb_ref[...], (8, height))

    @pl.loop(0, depth // 8)
    def _(i):
        rows = pl.ds(pl.multiple_of(i * 8, 8), 8)
        later = jnp.zeros((8, height), F32)
        entered = entered_ref[rows, :]
        for b in reversed(range(beam)):
            back = back_ref[b : b + 1, :]
            known_ref[b, rows, :] = entered * (absorb * later - back * light_ref[b, rows, :])
            later = later + back * emit_ref[b, rows, :]


def final_body(mine_ref, other_ref, absorb_ref, known_ref, out_hbm, after_ref, out_ref, sems):
    beam = known_ref.shape[0]
    step = beam // CHUNKS
    after = joined(after_ref, mine_ref[...], other_ref[...]) * absorb_ref[...]
    copies = []
    for k in range(CHUNKS):
        for b in range(k * step, (k + 1) * step):
            out_ref[b] = known_ref[b] + after
        part = pl.ds(k * step, step)
        copy = pltpu.make_async_copy(out_ref.at[part], out_hbm.at[part], sems.at[k])
        copy.start()
        copies.append(copy)
    for copy in copies:
        copy.wait()


def scanned(mine, other, flags, reverse):
    if reverse:
        flags = 1.0 - flags
    late_z, late_core = flags[0:1], flags[1:2]
    partner = lax.ppermute(other, "core", xor(2, 1))
    pair = mine + partner
    rows = [lax.ppermute(pair, "x", xor(4, k)) for k in (1, 2, 3)]
    over_x = flags[2:3] * rows[0] + flags[3:4] * rows[1] + flags[4:5] * rows[2]
    sent = over_x + (1.0 - late_z) * pair
    crossed = lax.ppermute(sent, "zh", xor(2, 1))
    base = over_x + crossed
    for_me = base + late_core * partner
    for_other = base + (1.0 - late_core) * mine
    return for_me, lax.ppermute(for_other, "core", xor(2, 1))


def local(concentration, entry_intensity, absorb, blur_taps, measured):
    beam, depth, height = concentration.shape
    depth_count = lax.axis_size("y") * lax.axis_size("zl")
    scale = 1.0 / (depth * depth_count)
    width = height // depth_count
    block = pltpu.VMEM((beam, depth, height), F32)
    plane = jax.ShapeDtypeStruct((depth, height), F32)
    half = jax.ShapeDtypeStruct((depth // 2, height), F32)
    camera = jax.ShapeDtypeStruct((beam, height), F32)
    size = beam * depth * height
    rate = absorb.reshape(1, height)
    scratch_plane = pltpu.VMEM((depth, height), F32)

    cells, mine, other, flags = call(
        load_body, (block, half, half, jax.ShapeDtypeStruct((8, height), F32)), [HBM], (VM,) * 4, size, 8 * size,
        scratch=(scratch_plane, pltpu.SemaphoreType.DMA((CHUNKS,))),
    )(pltpu.with_memory_space_constraint(concentration, pltpu.HBM))
    light, emit = call(local_body, (block, block), [VM, VM], (VM, VM), 4 * size, 12 * size, size)(cells, rate)
    before_mine, before_other = scanned(mine, other, flags, False)
    entered, part = call(
        image_body, (plane, camera), [VM] * 5, (VM, VM), 2 * size, 4 * size, depth * height, scratch=(scratch_plane,)
    )(before_mine, before_other, rate, entry_intensity, emit)

    over_y = part
    for k in (1, 2, 3):
        over_y = over_y + lax.ppermute(part, "y", xor(4, k))
    sums = [over_y] + [lax.ppermute(over_y, "zl", xor(4, k)) for k in (1, 2, 3)]

    def adjoint(*refs):
        adjoint_body(scale, *refs)

    full_residual, back, mine, other = call(
        adjoint, (camera, camera, half, half), [VM] * 4 + [SM] + [VM] * 3, (VM,) * 4, 2 * size, 4 * size,
        scratch=(scratch_plane,),
    )(*sums, blur_taps, measured, emit, entered)
    known, columns = call(
        partial_body, (block, jax.ShapeDtypeStruct((width, beam), F32)), [VM] * 6, (VM, VM),
        6 * size, 12 * size, scratch=(pltpu.VMEM((height, beam), F32),),
    )(rate, back, full_residual, entered, light, emit)
    after_mine, after_other = scanned(mine, other, flags, True)
    descent = call(
        final_body, jax.ShapeDtypeStruct((beam, depth, height), F32), [VM] * 4, HBM, size, 12 * size,
        scratch=(scratch_plane, pltpu.VMEM((beam, depth, height), F32), pltpu.SemaphoreType.DMA((CHUNKS,))),
    )(after_mine, after_other, rate, known)
    return descent, columns.T


def solution(mesh):
    finer = Mesh(mesh.devices.reshape(4, 2, 2, 4, 4), BEAM + DEPTH)
    placed = (P(BEAM, DEPTH, None), P(DEPTH, None), P(), P(), P(BEAM, None))
    return jax.shard_map(
        local,
        mesh=finer,
        in_specs=placed,
        out_specs=(P(BEAM, DEPTH, None), P(BEAM, DEPTH)),
        check_vma=False,
    )
```

profile of v0, /device:TPU:1, one launch (start us, length us, event | category | flops | bytes accessed | tf_op | source)
XLA Modules:
  0.0 67.8 jit_solution(4574501308110208061)
XLA Ops:
  0.6 0.0 copy-start.2
  0.6 0.0 copy-start
  0.6 2.3 %shard_map.68 = (f32[32,128,256]{2,1,0:T(8,128)S(1)}, f32[64,256]{1,0:T(8,128)S(1)}, f32[64,256]{1,0:T(8,128)S(1)}, f32[8,256]{1,0:T(8,128)S(1)}) custom-call(f32[32,128,256]{2,1,0:T(8,128)} %c_hbm.1), custom_call_target="tpu_custom_call" | custom-call | flops 1048576 | bytes 8388608 | tf_op jit(solution)/shard_map/pallas_call | solution.py:192
  3.0 3.3 %collective-permute-start = (f32[64,256]{1,0:T(8,128)S(1)}, f32[64,256]{1,0:T(8,128)S(1)}, u32[]{:S(2)}, u32[]{:S(2)}) collective-permute-start(f32[64,256]{1,0:T(8,128)S(1)} %get-tuple-element.18), channel_id=1, source_target_pairs={{0,16},{16,0},{1,17},{17,1},{2,18},{18,2},{3,19},{19,3},{4,20},{20... | collective-permute-start | bytes 196616 | tf_op jit(solution)/shard_map/ppermute | solution.py:167
  6.2 0.9 %collective-permute-done = f32[64,256]{1,0:T(8,128)S(1)} collective-permute-done((f32[64,256]{1,0:T(8,128)S(1)}, f32[64,256]{1,0:T(8,128)S(1)}, u32[]{:S(2)}, u32[]{:S(2)}) %collective-permute-start) | collective-permute-done | bytes 65568 | tf_op jit(solution)/shard_map/ppermute | solution.py:167
  7.2 0.9 %collective-permute-start.3 = (f32[64,256]{1,0:T(8,128)S(1)}, f32[64,256]{1,0:T(8,128)S(1)}, u32[]{:S(2)}, u32[]{:S(2)}) collective-permute-start(f32[64,256]{1,0:T(8,128)S(1)} %add.51), channel_id=1, source_target_pairs={{0,192},{64,128},{128,64},{192,0},{1,193},{65,129},{129,65},{193,1... | collective-permute-start | bytes 196616 | tf_op jit(solution)/shard_map/ppermute | solution.py:169
  8.0 0.5 collective-permute-start.2
  8.5 2.0 %collective-permute-start.1 = (f32[64,256]{1,0:T(8,128)S(1)}, f32[64,256]{1,0:T(8,128)S(1)}, u32[]{:S(2)}, u32[]{:S(2)}) collective-permute-start(f32[64,256]{1,0:T(8,128)S(1)} %add.51), channel_id=1, source_target_pairs={{0,64},{64,0},{128,192},{192,128},{1,65},{65,1},{129,193},{193,129... | collective-permute-start | bytes 196616 | tf_op jit(solution)/shard_map/ppermute | solution.py:169
  10.5 1.1 %collective-permute-done.3 = f32[64,256]{1,0:T(8,128)S(1)} collective-permute-done((f32[64,256]{1,0:T(8,128)S(1)}, f32[64,256]{1,0:T(8,128)S(1)}, u32[]{:S(2)}, u32[]{:S(2)}) %collective-permute-start.3) | collective-permute-done | bytes 65568 | tf_op jit(solution)/shard_map/ppermute | solution.py:169
  11.6 1.2 %collective-permute-done.2 = f32[64,256]{1,0:T(8,128)S(1)} collective-permute-done((f32[64,256]{1,0:T(8,128)S(1)}, f32[64,256]{1,0:T(8,128)S(1)}, u32[]{:S(2)}, u32[]{:S(2)}) %collective-permute-start.2) | collective-permute-done | bytes 65568 | tf_op jit(solution)/shard_map/ppermute | solution.py:169
  12.7 0.7 %collective-permute-done.1 = f32[64,256]{1,0:T(8,128)S(1)} collective-permute-done((f32[64,256]{1,0:T(8,128)S(1)}, f32[64,256]{1,0:T(8,128)S(1)}, u32[]{:S(2)}, u32[]{:S(2)}) %collective-permute-start.1) | collective-permute-done | bytes 65568 | tf_op jit(solution)/shard_map/ppermute | solution.py:169
  13.5 6.2 %collective-permute-start.4 = (f32[64,256]{1,0:T(8,128)S(1)}, f32[64,256]{1,0:T(8,128)S(1)}, u32[]{:S(2)}, u32[]{:S(2)}) collective-permute-start(f32[64,256]{1,0:T(8,128)S(1)} %get-tuple-element.32), channel_id=1, source_target_pairs={{0,32},{32,0},{1,33},{33,1},{2,34},{34,2},{3,35},{35,3},{4,36},{36... | collective-permute-start | bytes 196616 | tf_op jit(solution)/shard_map/ppermute | solution.py:172
  19.7 1.7 %collective-permute-done.4 = f32[64,256]{1,0:T(8,128)S(1)} collective-permute-done((f32[64,256]{1,0:T(8,128)S(1)}, f32[64,256]{1,0:T(8,128)S(1)}, u32[]{:S(2)}, u32[]{:S(2)}) %collective-permute-start.4) | collective-permute-done | bytes 65568 | tf_op jit(solution)/shard_map/ppermute | solution.py:172
  21.4 3.1 %collective-permute-start.5 = (f32[64,256]{1,0:T(8,128)S(1)}, f32[64,256]{1,0:T(8,128)S(1)}, u32[]{:S(2)}, u32[]{:S(2)}) collective-permute-start(f32[64,256]{1,0:T(8,128)S(1)} %get-tuple-element.36), channel_id=1, source_target_pairs={{0,16},{16,0},{1,17},{17,1},{2,18},{18,2},{3,19},{19,3},{4,20},{20... | collective-permute-start | bytes 196616 | tf_op jit(solution)/shard_map/ppermute | solution.py:176
  24.5 0.0 copy-done.2
  24.5 0.0 copy-start.1
  24.5 0.0 copy-start.3
  24.5 0.8 %shard_map.69 = (f32[32,128,256]{2,1,0:T(8,128)S(1)}, f32[32,128,256]{2,1,0:T(8,128)S(1)}) custom-call(f32[32,128,256]{2,1,0:T(8,128)S(1)} %get-tuple-element.19.c_ref, f32[1,256]{1,0:T(1,128)S(1)} %bitcast.14), custom_call_target="tpu_custom_call" | custom-call | flops 4194304 | bytes 12582912 | tf_op jit(solution)/shard_map/pallas_call | solution.py:196
  25.3 0.1 collective-permute-done.5.other_ref
  25.4 0.0 copy-done
  25.4 0.4 shard_map.70
  25.8 2.8 %collective-permute-start.8 = (f32[32,256]{1,0:T(8,128)S(1)}, f32[32,256]{1,0:T(8,128)S(1)}, u32[]{:S(2)}, u32[]{:S(2)}) collective-permute-start(f32[32,256]{1,0:T(8,128)S(1)} %get-tuple-element.21), channel_id=1, source_target_pairs={{0,12},{4,8},{8,4},{12,0},{1,13},{5,9},{9,5},{13,1},{2,14},{6,10},... | collective-permute-start | bytes 98312 | tf_op jit(solution)/shard_map/ppermute | solution.py:204
  28.6 0.3 collective-permute-start.7
  29.0 0.3 collective-permute-start.6
  29.3 0.6 collective-permute-done.8
  29.9 3.0 %collective-permute-done.7 = f32[32,256]{1,0:T(8,128)S(1)} collective-permute-done((f32[32,256]{1,0:T(8,128)S(1)}, f32[32,256]{1,0:T(8,128)S(1)}, u32[]{:S(2)}, u32[]{:S(2)}) %collective-permute-start.7) | collective-permute-done | bytes 32800 | tf_op jit(solution)/shard_map/ppermute | solution.py:204
  32.9 0.0 collective-permute-done.6
  32.9 1.2 %collective-permute-start.9 = (f32[32,256]{1,0:T(8,128)S(1)}, f32[32,256]{1,0:T(8,128)S(1)}, u32[]{:S(2)}, u32[]{:S(2)}) collective-permute-start(f32[32,256]{1,0:T(8,128)S(1)} %add_add_fusion.refs_0_), channel_id=1, source_target_pairs={{0,1},{1,0},{2,3},{3,2},{4,5},{5,4},{6,7},{7,6},{8,9},{9,8},{10,11... | collective-permute-start | bytes 98312 | tf_op jit(solution)/shard_map/ppermute | solution.py:205
  34.1 2.8 %collective-permute-start.10 = (f32[32,256]{1,0:T(8,128)S(1)}, f32[32,256]{1,0:T(8,128)S(1)}, u32[]{:S(2)}, u32[]{:S(2)}) collective-permute-start(f32[32,256]{1,0:T(8,128)S(1)} %add_add_fusion.refs_0_), channel_id=1, source_target_pairs={{0,2},{1,3},{2,0},{3,1},{4,6},{5,7},{6,4},{7,5},{8,10},{9,11},{10,... | collective-permute-start | bytes 98312 | tf_op jit(solution)/shard_map/ppermute | solution.py:205
  37.0 0.0 collective-permute-start.11
  37.0 0.0 collective-permute-done.9.refs_1_
  37.0 1.6 %collective-permute-done.10.refs_2_ = f32[32,256]{1,0:T(8,128)S(1)} collective-permute-done((f32[32,256]{1,0:T(8,128)S(1)}, f32[32,256]{1,0:T(8,128)S(1)}, u32[]{:S(2)}, u32[]{:S(2)}) %collective-permute-start.10) | collective-permute-done | bytes 32800 | tf_op jit(solution)/shard_map/ppermute | solution.py:205
  38.6 2.9 %collective-permute-done.11.refs_3_ = f32[32,256]{1,0:T(8,128)S(1)} collective-permute-done((f32[32,256]{1,0:T(8,128)S(1)}, f32[32,256]{1,0:T(8,128)S(1)}, u32[]{:S(2)}, u32[]{:S(2)}) %collective-permute-start.11) | collective-permute-done | bytes 32800 | tf_op jit(solution)/shard_map/ppermute | solution.py:205
  41.5 0.0 copy-done.1
  41.5 0.0 copy-done.3
  41.5 1.1 %shard_map.71 = (f32[32,256]{1,0:T(8,128)S(1)}, f32[32,256]{1,0:T(8,128)S(1)}, f32[64,256]{1,0:T(8,128)S(1)}, f32[64,256]{1,0:T(8,128)S(1)}) custom-call(f32[32,256]{1,0:T(8,128)S(1)} %add_add_fusion.refs_0_, f32[32,256]{1,0:T(8,128)S(1)} %collective-permute-done.9.refs_1_, f32[32,256]{1,0:T(8,128)S(1)} %collective-permute-done.10.refs_2_, ...), custom_call_target="tpu_custom_call" | custom-call | flops 2097152 | bytes 4194304 | tf_op jit(solution)/shard_map/pallas_call | solution.py:210
  42.7 3.6 %collective-permute-start.12 = (f32[64,256]{1,0:T(8,128)S(1)}, f32[64,256]{1,0:T(8,128)S(1)}, u32[]{:S(2)}, u32[]{:S(2)}) collective-permute-start(f32[64,256]{1,0:T(8,128)S(1)} %get-tuple-element.24), channel_id=1, source_target_pairs={{0,16},{16,0},{1,17},{17,1},{2,18},{18,2},{3,19},{19,3},{4,20},{20... | collective-permute-start | bytes 196616 | tf_op jit(solution)/shard_map/ppermute | solution.py:167
  46.3 0.9 %collective-permute-done.12 = f32[64,256]{1,0:T(8,128)S(1)} collective-permute-done((f32[64,256]{1,0:T(8,128)S(1)}, f32[64,256]{1,0:T(8,128)S(1)}, u32[]{:S(2)}, u32[]{:S(2)}) %collective-permute-start.12) | collective-permute-done | bytes 65568 | tf_op jit(solution)/shard_map/ppermute | solution.py:167
  47.2 0.4 collective-permute-start.15
  47.5 1.7 %collective-permute-start.14 = (f32[64,256]{1,0:T(8,128)S(1)}, f32[64,256]{1,0:T(8,128)S(1)}, u32[]{:S(2)}, u32[]{:S(2)}) collective-permute-start(f32[64,256]{1,0:T(8,128)S(1)} %add.61), channel_id=1, source_target_pairs={{0,128},{64,192},{128,0},{192,64},{1,129},{65,193},{129,1},{193,65... | collective-permute-start | bytes 196616 | tf_op jit(solution)/shard_map/ppermute | solution.py:169
  49.2 1.3 %collective-permute-start.13 = (f32[64,256]{1,0:T(8,128)S(1)}, f32[64,256]{1,0:T(8,128)S(1)}, u32[]{:S(2)}, u32[]{:S(2)}) collective-permute-start(f32[64,256]{1,0:T(8,128)S(1)} %add.61), channel_id=1, source_target_pairs={{0,64},{64,0},{128,192},{192,128},{1,65},{65,1},{129,193},{193,129... | collective-permute-start | bytes 196616 | tf_op jit(solution)/shard_map/ppermute | solution.py:169
  50.5 2.1 %collective-permute-done.15 = f32[64,256]{1,0:T(8,128)S(1)} collective-permute-done((f32[64,256]{1,0:T(8,128)S(1)}, f32[64,256]{1,0:T(8,128)S(1)}, u32[]{:S(2)}, u32[]{:S(2)}) %collective-permute-start.15) | collective-permute-done | bytes 65568 | tf_op jit(solution)/shard_map/ppermute | solution.py:169
  52.6 0.0 collective-permute-done.14
  52.6 0.9 %collective-permute-done.13 = f32[64,256]{1,0:T(8,128)S(1)} collective-permute-done((f32[64,256]{1,0:T(8,128)S(1)}, f32[64,256]{1,0:T(8,128)S(1)}, u32[]{:S(2)}, u32[]{:S(2)}) %collective-permute-start.13) | collective-permute-done | bytes 65568 | tf_op jit(solution)/shard_map/ppermute | solution.py:169
  53.5 3.5 %collective-permute-start.16 = (f32[64,256]{1,0:T(8,128)S(1)}, f32[64,256]{1,0:T(8,128)S(1)}, u32[]{:S(2)}, u32[]{:S(2)}) collective-permute-start(f32[64,256]{1,0:T(8,128)S(1)} %get-tuple-element.30), channel_id=1, source_target_pairs={{0,32},{32,0},{1,33},{33,1},{2,34},{34,2},{3,35},{35,3},{4,36},{36... | collective-permute-start | bytes 196616 | tf_op jit(solution)/shard_map/ppermute | solution.py:172
  57.0 4.3 %collective-permute-done.16 = f32[64,256]{1,0:T(8,128)S(1)} collective-permute-done((f32[64,256]{1,0:T(8,128)S(1)}, f32[64,256]{1,0:T(8,128)S(1)}, u32[]{:S(2)}, u32[]{:S(2)}) %collective-permute-start.16) | collective-permute-done | bytes 65568 | tf_op jit(solution)/shard_map/ppermute | solution.py:172
  61.3 2.7 %collective-permute-start.17 = (f32[64,256]{1,0:T(8,128)S(1)}, f32[64,256]{1,0:T(8,128)S(1)}, u32[]{:S(2)}, u32[]{:S(2)}) collective-permute-start(f32[64,256]{1,0:T(8,128)S(1)} %get-tuple-element.34), channel_id=1, source_target_pairs={{0,16},{16,0},{1,17},{17,1},{2,18},{18,2},{3,19},{19,3},{4,20},{20... | collective-permute-start | bytes 196616 | tf_op jit(solution)/shard_map/ppermute | solution.py:176
  64.0 1.7 %shard_map.72 = (f32[32,128,256]{2,1,0:T(8,128)S(1)}, f32[16,32]{1,0:T(8,128)}) custom-call(f32[1,256]{1,0:T(1,128)S(1)} %bitcast.16, f32[32,256]{1,0:T(8,128)S(1)} %get-tuple-element.25.back_ref, f32[32,256]{1,0:T(8,128)S(1)} %get-tuple-element.26.residual_ref, f32[128,256]{1,0:T(8,128)S(1)} %get-tuple-element.22.refs_7_.entered_ref, ...), custom_call_target="tpu_custom_call" | custom-call | flops 6291456 | bytes 12582912 | tf_op jit(solution)/shard_map/pallas_call | solution.py:214
  65.7 0.0 collective-permute-done.17.other_ref
  65.7 2.1 %shard_map.73 = f32[32,128,256]{2,1,0:T(8,128)} custom-call(f32[64,256]{1,0:T(8,128)S(1)} %get-tuple-element.35.mine_ref, f32[64,256]{1,0:T(8,128)S(1)} %collective-permute-done.17.other_ref, f32[1,256]{1,0:T(1,128)S(1)} %bitcast.17, f32[32,128,256]{2,1,0:T(8,128)S(1)} %get-tuple-element.28.known_ref), custom_call_target="tpu_custom_call" | custom-call | flops 1048576 | bytes 12582912 | tf_op jit(solution)/shard_map/pallas_call | solution.py:219
  (10 shorter events, 0.1 us)
Async XLA Ops:
  0.6 23.9 %copy-start.2 = (f32[256]{0:T(256)S(1)}, f32[256]{0:T(256)}, u32[]{:S(2)}) copy-start(f32[256]{0:T(256)} %param.7) | copy-start | bytes 3076
  0.6 24.8 %copy-start = (f32[128,256]{1,0:T(8,128)S(1)}, f32[128,256]{1,0:T(8,128)}, u32[]{:S(2)}) copy-start(f32[128,256]{1,0:T(8,128)} %entry_ref.1) | copy-start | bytes 393220
  3.0 4.2 %collective-permute-start = (f32[64,256]{1,0:T(8,128)S(1)}, f32[64,256]{1,0:T(8,128)S(1)}, u32[]{:S(2)}, u32[]{:S(2)}) collective-permute-start(f32[64,256]{1,0:T(8,128)S(1)} %get-tuple-element.18), channel_id=1, source_target_pairs={{0,16},{16,0},{1,17},{17,1},{2,18},{18,2},{3,19},{19,3},{4,20},{20... | collective-permute-start | bytes 196616 | tf_op jit(solution)/shard_map/ppermute | solution.py:167
  7.2 4.4 %collective-permute-start.3 = (f32[64,256]{1,0:T(8,128)S(1)}, f32[64,256]{1,0:T(8,128)S(1)}, u32[]{:S(2)}, u32[]{:S(2)}) collective-permute-start(f32[64,256]{1,0:T(8,128)S(1)} %add.51), channel_id=1, source_target_pairs={{0,192},{64,128},{128,64},{192,0},{1,193},{65,129},{129,65},{193,1... | collective-permute-start | bytes 196616 | tf_op jit(solution)/shard_map/ppermute | solution.py:169
  8.0 4.7 %collective-permute-start.2 = (f32[64,256]{1,0:T(8,128)S(1)}, f32[64,256]{1,0:T(8,128)S(1)}, u32[]{:S(2)}, u32[]{:S(2)}) collective-permute-start(f32[64,256]{1,0:T(8,128)S(1)} %add.51), channel_id=1, source_target_pairs={{0,128},{64,192},{128,0},{192,64},{1,129},{65,193},{129,1},{193,65... | collective-permute-start | bytes 196616 | tf_op jit(solution)/shard_map/ppermute | solution.py:169
  8.5 4.9 %collective-permute-start.1 = (f32[64,256]{1,0:T(8,128)S(1)}, f32[64,256]{1,0:T(8,128)S(1)}, u32[]{:S(2)}, u32[]{:S(2)}) collective-permute-start(f32[64,256]{1,0:T(8,128)S(1)} %add.51), channel_id=1, source_target_pairs={{0,64},{64,0},{128,192},{192,128},{1,65},{65,1},{129,193},{193,129... | collective-permute-start | bytes 196616 | tf_op jit(solution)/shard_map/ppermute | solution.py:169
  13.5 7.9 %collective-permute-start.4 = (f32[64,256]{1,0:T(8,128)S(1)}, f32[64,256]{1,0:T(8,128)S(1)}, u32[]{:S(2)}, u32[]{:S(2)}) collective-permute-start(f32[64,256]{1,0:T(8,128)S(1)} %get-tuple-element.32), channel_id=1, source_target_pairs={{0,32},{32,0},{1,33},{33,1},{2,34},{34,2},{3,35},{35,3},{4,36},{36... | collective-permute-start | bytes 196616 | tf_op jit(solution)/shard_map/ppermute | solution.py:172
  21.4 4.0 %collective-permute-start.5 = (f32[64,256]{1,0:T(8,128)S(1)}, f32[64,256]{1,0:T(8,128)S(1)}, u32[]{:S(2)}, u32[]{:S(2)}) collective-permute-start(f32[64,256]{1,0:T(8,128)S(1)} %get-tuple-element.36), channel_id=1, source_target_pairs={{0,16},{16,0},{1,17},{17,1},{2,18},{18,2},{3,19},{19,3},{4,20},{20... | collective-permute-start | bytes 196616 | tf_op jit(solution)/shard_map/ppermute | solution.py:176
  24.5 17.0 %copy-start.1 = (f32[32,256]{1,0:T(8,128)S(1)}, f32[32,256]{1,0:T(8,128)}, u32[]{:S(2)}) copy-start(f32[32,256]{1,0:T(8,128)} %refs_5_.1) | copy-start | bytes 98308
  24.5 17.0 %copy-start.3 = (f32[5]{0:T(128)S(1)}, f32[5]{0:T(128)}, u32[]{:S(2)}) copy-start(f32[5]{0:T(128)} %refs_4_.1) | copy-start | bytes 64
  25.8 4.1 %collective-permute-start.8 = (f32[32,256]{1,0:T(8,128)S(1)}, f32[32,256]{1,0:T(8,128)S(1)}, u32[]{:S(2)}, u32[]{:S(2)}) collective-permute-start(f32[32,256]{1,0:T(8,128)S(1)} %get-tuple-element.21), channel_id=1, source_target_pairs={{0,12},{4,8},{8,4},{12,0},{1,13},{5,9},{9,5},{13,1},{2,14},{6,10},... | collective-permute-start | bytes 98312 | tf_op jit(solution)/shard_map/ppermute | solution.py:204
  28.6 4.3 %collective-permute-start.7 = (f32[32,256]{1,0:T(8,128)S(1)}, f32[32,256]{1,0:T(8,128)S(1)}, u32[]{:S(2)}, u32[]{:S(2)}) collective-permute-start(f32[32,256]{1,0:T(8,128)S(1)} %get-tuple-element.21), channel_id=1, source_target_pairs={{0,8},{4,12},{8,0},{12,4},{1,9},{5,13},{9,1},{13,5},{2,10},{6,14},... | collective-permute-start | bytes 98312 | tf_op jit(solution)/shard_map/ppermute | solution.py:204
  29.0 3.9 %collective-permute-start.6 = (f32[32,256]{1,0:T(8,128)S(1)}, f32[32,256]{1,0:T(8,128)S(1)}, u32[]{:S(2)}, u32[]{:S(2)}) collective-permute-start(f32[32,256]{1,0:T(8,128)S(1)} %get-tuple-element.21), channel_id=1, source_target_pairs={{0,4},{4,0},{8,12},{12,8},{1,5},{5,1},{9,13},{13,9},{2,6},{6,2},{1... | collective-permute-start | bytes 98312 | tf_op jit(solution)/shard_map/ppermute | solution.py:204
  32.9 4.1 %collective-permute-start.9 = (f32[32,256]{1,0:T(8,128)S(1)}, f32[32,256]{1,0:T(8,128)S(1)}, u32[]{:S(2)}, u32[]{:S(2)}) collective-permute-start(f32[32,256]{1,0:T(8,128)S(1)} %add_add_fusion.refs_0_), channel_id=1, source_target_pairs={{0,1},{1,0},{2,3},{3,2},{4,5},{5,4},{6,7},{7,6},{8,9},{9,8},{10,11... | collective-permute-start | bytes 98312 | tf_op jit(solution)/shard_map/ppermute | solution.py:205
  34.1 4.5 %collective-permute-start.10 = (f32[32,256]{1,0:T(8,128)S(1)}, f32[32,256]{1,0:T(8,128)S(1)}, u32[]{:S(2)}, u32[]{:S(2)}) collective-permute-start(f32[32,256]{1,0:T(8,128)S(1)} %add_add_fusion.refs_0_), channel_id=1, source_target_pairs={{0,2},{1,3},{2,0},{3,1},{4,6},{5,7},{6,4},{7,5},{8,10},{9,11},{10,... | collective-permute-start | bytes 98312 | tf_op jit(solution)/shard_map/ppermute | solution.py:205
  37.0 4.6 %collective-permute-start.11 = (f32[32,256]{1,0:T(8,128)S(1)}, f32[32,256]{1,0:T(8,128)S(1)}, u32[]{:S(2)}, u32[]{:S(2)}) collective-permute-start(f32[32,256]{1,0:T(8,128)S(1)} %add_add_fusion.refs_0_), channel_id=1, source_target_pairs={{0,3},{1,2},{2,1},{3,0},{4,7},{5,6},{6,5},{7,4},{8,11},{9,10},{10,... | collective-permute-start | bytes 98312 | tf_op jit(solution)/shard_map/ppermute | solution.py:205
  42.7 4.5 %collective-permute-start.12 = (f32[64,256]{1,0:T(8,128)S(1)}, f32[64,256]{1,0:T(8,128)S(1)}, u32[]{:S(2)}, u32[]{:S(2)}) collective-permute-start(f32[64,256]{1,0:T(8,128)S(1)} %get-tuple-element.24), channel_id=1, source_target_pairs={{0,16},{16,0},{1,17},{17,1},{2,18},{18,2},{3,19},{19,3},{4,20},{20... | collective-permute-start | bytes 196616 | tf_op jit(solution)/shard_map/ppermute | solution.py:167
  47.2 5.4 %collective-permute-start.15 = (f32[64,256]{1,0:T(8,128)S(1)}, f32[64,256]{1,0:T(8,128)S(1)}, u32[]{:S(2)}, u32[]{:S(2)}) collective-permute-start(f32[64,256]{1,0:T(8,128)S(1)} %add.61), channel_id=1, source_target_pairs={{0,192},{64,128},{128,64},{192,0},{1,193},{65,129},{129,65},{193,1... | collective-permute-start | bytes 196616 | tf_op jit(solution)/shard_map/ppermute | solution.py:169
  47.5 5.1 %collective-permute-start.14 = (f32[64,256]{1,0:T(8,128)S(1)}, f32[64,256]{1,0:T(8,128)S(1)}, u32[]{:S(2)}, u32[]{:S(2)}) collective-permute-start(f32[64,256]{1,0:T(8,128)S(1)} %add.61), channel_id=1, source_target_pairs={{0,128},{64,192},{128,0},{192,64},{1,129},{65,193},{129,1},{193,65... | collective-permute-start | bytes 196616 | tf_op jit(solution)/shard_map/ppermute | solution.py:169
  49.2 4.3 %collective-permute-start.13 = (f32[64,256]{1,0:T(8,128)S(1)}, f32[64,256]{1,0:T(8,128)S(1)}, u32[]{:S(2)}, u32[]{:S(2)}) collective-permute-start(f32[64,256]{1,0:T(8,128)S(1)} %add.61), channel_id=1, source_target_pairs={{0,64},{64,0},{128,192},{192,128},{1,65},{65,1},{129,193},{193,129... | collective-permute-start | bytes 196616 | tf_op jit(solution)/shard_map/ppermute | solution.py:169
  53.5 7.8 %collective-permute-start.16 = (f32[64,256]{1,0:T(8,128)S(1)}, f32[64,256]{1,0:T(8,128)S(1)}, u32[]{:S(2)}, u32[]{:S(2)}) collective-permute-start(f32[64,256]{1,0:T(8,128)S(1)} %get-tuple-element.30), channel_id=1, source_target_pairs={{0,32},{32,0},{1,33},{33,1},{2,34},{34,2},{3,35},{35,3},{4,36},{36... | collective-permute-start | bytes 196616 | tf_op jit(solution)/shard_map/ppermute | solution.py:172
  61.3 4.4 %collective-permute-start.17 = (f32[64,256]{1,0:T(8,128)S(1)}, f32[64,256]{1,0:T(8,128)S(1)}, u32[]{:S(2)}, u32[]{:S(2)}) collective-permute-start(f32[64,256]{1,0:T(8,128)S(1)} %get-tuple-element.34), channel_id=1, source_target_pairs={{0,16},{16,0},{1,17},{17,1},{2,18},{18,2},{3,19},{19,3},{4,20},{20... | collective-permute-start | bytes 196616 | tf_op jit(solution)/shard_map/ppermute | solution.py:176
where the time goes:
time: 67.9 us; the launch traced here: 67.8 us
  starting transfers between devices  36.6 us (54%)
  waiting for transfers between devices  22 us (32%)
  Pallas kernels  8.41 us (12%)
  between operations  0.71 us (1%)
    ppermute x2, starting transfers between devices, scanned(): crossed = lax.ppermute(sent, 'zh', xor(2, 1))  9.71 us
    ppermute x2, starting transfers between devices, scanned(): partner = lax.ppermute(other, 'core', xor(2, 1))  6.86 us
    ppermute x6, starting transfers between devices, scanned(): rows = [lax.ppermute(pair, 'x', xor(4, k)) for k in (1, 2, 3)]  6.68 us
    ppermute x2, waiting for transfers between devices, scanned(): crossed = lax.ppermute(sent, 'zh', xor(2, 1))  6.01 us
    ppermute x6, waiting for transfers between devices, scanned(): rows = [lax.ppermute(pair, 'x', xor(4, k)) for k in (1, 2, 3)]  5.89 us
    ppermute x2, starting transfers between devices, scanned(): return (for_me, lax.ppermute(for_other, 'core', xor(2, 1)))  5.81 us
    ppermute x3, waiting for transfers between devices, local(): sums = [over_y] + [lax.ppermute(over_y, 'zl', xor(4, k)) for k in (1, 2, 3)]  4.56 us
    ppermute x3, starting transfers between devices, local(): sums = [over_y] + [lax.ppermute(over_y, 'zl', xor(4, k)) for k in (1, 2, 3)]  4.05 us
  transfers between devices with their start and end apart: 18, of which 14 were waited for; matrix products, arithmetic and copies ran while one was open for 0% of the time, Pallas kernels for 4%

commit v1 on v0

v1 whole, which is shorter than its diff:
```python
import jax
import jax.numpy as jnp
from jax import lax
from jax.experimental import pallas as pl
from jax.experimental.pallas import tpu as pltpu
from jax.sharding import Mesh
from jax.sharding import PartitionSpec as P

BEAM = ("x", "zh", "core")
DEPTH = ("y", "zl")
LOG2E = 1.4426950408889634
CHUNKS = 8
VM = pl.BlockSpec(memory_space=pltpu.VMEM)
SM = pl.BlockSpec(memory_space=pltpu.SMEM)
HBM = pl.BlockSpec(memory_space=pltpu.HBM)
F32 = jnp.float32


def xor(count, bits):
    return [(i, i ^ bits) for i in range(count)]


def call(body, outs, in_specs, out_specs, flops, nbytes, exps=0, scratch=(), aliases=None):
    return pl.pallas_call(
        body,
        out_shape=outs,
        in_specs=in_specs,
        out_specs=out_specs,
        scratch_shapes=scratch,
        input_output_aliases=aliases or {},
        cost_estimate=pl.CostEstimate(flops=flops, bytes_accessed=nbytes, transcendentals=exps),
        compiler_params=pltpu.CompilerParams(vmem_limit_bytes=8 * 2**20),
    )


def half_rows(own, count):
    core = lax.axis_index("core")
    return pl.ds(pl.multiple_of((core if own else 1 - core) * count, 8), count)


def loaded(own, c_hbm, c_ref, total_ref, sems):
    beam, count, _ = c_ref.shape
    rows = half_rows(own, count)
    step = beam // CHUNKS
    copies = []
    for k in range(CHUNKS):
        part = pl.ds(k * step, step)
        copy = pltpu.make_async_copy(c_hbm.at[part, rows], c_ref.at[part], sems.at[k])
        copy.start()
        copies.append(copy)
    total = None
    for k in range(CHUNKS):
        copies[k].wait()
        part = jnp.sum(c_ref[k * step : (k + 1) * step], axis=0)
        total = part if total is None else total + part
    total_ref[...] = total


def load_other_body(c_hbm, c_ref, total_ref, flag_ref, sems):
    loaded(False, c_hbm, c_ref, total_ref, sems)
    x, zh, core = (lax.axis_index(name) for name in BEAM)
    flags = [zh, core] + [((x ^ k) < x).astype(jnp.int32) for k in (1, 2, 3)]
    for k, flag in enumerate(flags):
        flag_ref[k : k + 1, :] = jnp.full((1, flag_ref.shape[1]), flag.astype(F32))


def load_own_body(c_hbm, c_ref, total_ref, sems):
    loaded(True, c_hbm, c_ref, total_ref, sems)


def local_body(own_ref, other_ref, absorb_ref, light_ref, emit_ref):
    beam, count, height = own_ref.shape
    rate = jnp.broadcast_to(absorb_ref[...] * (-LOG2E), (8, height))
    for half, c_ref in enumerate((own_ref, other_ref)):

        @pl.loop(0, count // 8)
        def _(i, half=half, c_ref=c_ref):
            rows = pl.ds(pl.multiple_of(i * 8, 8), 8)
            prior = jnp.zeros((8, height), F32)
            for b in range(beam):
                c = c_ref[b, rows, :]
                light = jnp.exp2(rate * prior)
                light_ref[half, b, rows, :] = light
                emit_ref[half, b, rows, :] = light * c
                prior = prior + c


def imaged(half, before_ref, absorb_ref, entry_ref, emit_ref, entered_ref, part_ref, earlier_ref=None):
    beam, count = emit_ref.shape[1:3]
    entry = entry_ref[half_rows(half == 0, count), :]
    entered = entry * jnp.exp2(before_ref[...] * (absorb_ref[...] * (-LOG2E)))
    entered_ref[...] = entered
    for b in range(beam):
        row = jnp.sum(entered * emit_ref[half, b], axis=0, keepdims=True)
        part_ref[b : b + 1, :] = row if earlier_ref is None else row + earlier_ref[b : b + 1, :]


def image_own_body(before_ref, absorb_ref, entry_ref, emit_ref, entered_ref, part_ref):
    imaged(0, before_ref, absorb_ref, entry_ref, emit_ref, entered_ref, part_ref)


def image_other_body(before_ref, absorb_ref, entry_ref, emit_ref, earlier_ref, entered_ref, part_ref):
    imaged(1, before_ref, absorb_ref, entry_ref, emit_ref, entered_ref, part_ref, earlier_ref)


def shifted(value, by):
    width = value.shape[1]
    source = lax.broadcasted_iota(jnp.int32, value.shape, 1) + by
    moved = pltpu.roll(value, (-by) % width, 1)
    return jnp.where((source >= 0) & (source < width), moved, 0.0)


def blurred(value, taps_ref, sign):
    terms = [taps_ref[k] * shifted(value, sign * (k - 2)) for k in (0, 1, 3, 4)]
    return (taps_ref[2] * value + (terms[0] + terms[1])) + (terms[2] + terms[3])


def weighed(half, back_ref, emit_ref, entered_ref):
    total = None
    for b in range(emit_ref.shape[1]):
        term = back_ref[b : b + 1, :] * emit_ref[half, b]
        total = term if total is None else total + term
    return total * entered_ref[...]


def adjoint_other_body(scale, s0, s1, s2, s3, taps_ref, measured_ref, emit_ref, entered_ref,
                       residual_ref, back_ref, total_ref):
    image = ((s0[...] + s1[...]) + (s2[...] + s3[...])) * scale
    residual = blurred(image, taps_ref, 1) - measured_ref[...]
    residual_ref[...] = residual
    back_ref[...] = blurred(residual, taps_ref, -1)
    total_ref[...] = weighed(1, back_ref, emit_ref, entered_ref)


def adjoint_own_body(back_ref, emit_ref, entered_ref, total_ref):
    total_ref[...] = weighed(0, back_ref, emit_ref, entered_ref)


def partial_body(absorb_ref, back_ref, residual_ref, own_entered_ref, other_entered_ref, light_ref, emit_ref,
                 known_ref, columns_ref, turned_ref):
    _, beam, count, height = light_ref.shape
    width = columns_ref.shape[0]
    section = (lax.axis_index("y") * lax.axis_size("zl") + lax.axis_index("zl")) * width
    turned_ref[...] = residual_ref[...].T
    columns_ref[...] = turned_ref[pl.ds(pl.multiple_of(section, 8), width), :]
    absorb = jnp.broadcast_to(absorb_ref[...], (8, height))
    for half, entered_ref in enumerate((own_entered_ref, other_entered_ref)):

        @pl.loop(0, count // 8)
        def _(i, half=half, entered_ref=entered_ref):
            rows = pl.ds(pl.multiple_of(i * 8, 8), 8)
            later = jnp.zeros((8, height), F32)
            entered = entered_ref[rows, :]
            for b in reversed(range(beam)):
                back = back_ref[b : b + 1, :]
                known_ref[half, b, rows, :] = entered * (absorb * later - back * light_ref[half, b, rows, :])
                later = later + back * emit_ref[half, b, rows, :]


def written(half, after_ref, absorb_ref, known_ref, out_hbm, out_ref, sems):
    beam, count = known_ref.shape[1:3]
    rows = half_rows(half == 0, count)
    step = beam // CHUNKS
    after = after_ref[...] * absorb_ref[...]
    copies = []
    for k in range(CHUNKS):
        for b in range(k * step, (k + 1) * step):
            out_ref[b] = known_ref[half, b] + after
        part = pl.ds(k * step, step)
        copy = pltpu.make_async_copy(out_ref.at[part], out_hbm.at[part, rows], sems.at[k])
        copy.start()
        copies.append(copy)
    for copy in copies:
        copy.wait()


def final_own_body(after_ref, absorb_ref, known_ref, out_hbm, out_ref, sems):
    written(0, after_ref, absorb_ref, known_ref, out_hbm, out_ref, sems)


def final_other_body(after_ref, absorb_ref, known_ref, begun_hbm, out_hbm, out_ref, sems):
    written(1, after_ref, absorb_ref, known_ref, out_hbm, out_ref, sems)


def scanned(own, partner, flags, reverse):
    if reverse:
        flags = 1.0 - flags
    late_z, late_core = flags[0:1], flags[1:2]
    pair = own + partner
    rows = [lax.ppermute(pair, "x", xor(4, k)) for k in (1, 2, 3)]
    over_x = flags[2:3] * rows[0] + flags[3:4] * rows[1] + flags[4:5] * rows[2]
    sent = over_x + (1.0 - late_z) * pair
    crossed = lax.ppermute(sent, "zh", xor(2, 1))
    base = over_x + crossed
    for_me = base + late_core * partner
    for_other = base + (1.0 - late_core) * own
    return for_me, lax.ppermute(for_other, "core", xor(2, 1))


def local(concentration, entry_intensity, absorb, blur_taps, measured):
    beam, depth, height = concentration.shape
    count = depth // 2
    depth_count = lax.axis_size("y") * lax.axis_size("zl")
    scale = 1.0 / (depth * depth_count)
    width = height // depth_count
    half_block = pltpu.VMEM((beam, count, height), F32)
    blocks = pltpu.VMEM((2, beam, count, height), F32)
    half = jax.ShapeDtypeStruct((count, height), F32)
    camera = jax.ShapeDtypeStruct((beam, height), F32)
    size = beam * depth * height
    rate = absorb.reshape(1, height)
    copied = pltpu.SemaphoreType.DMA((CHUNKS,))
    source = pltpu.with_memory_space_constraint(concentration, pltpu.HBM)

    other_cells, other, flags = call(
        load_other_body, (half_block, half, jax.ShapeDtypeStruct((8, height), F32)), [HBM], (VM,) * 3,
        size // 2, 4 * size, scratch=(copied,),
    )(source)
    partner = lax.ppermute(other, "core", xor(2, 1))
    own_cells, own = call(
        load_own_body, (half_block, half), [HBM], (VM, VM), size // 2, 4 * size, scratch=(copied,)
    )(source)
    light, emit = call(
        local_body, (blocks, blocks), [VM] * 3, (VM, VM), 4 * size, 12 * size, size
    )(own_cells, other_cells, rate)
    before_own, before_other = scanned(own, partner, flags, False)
    own_entered, part = call(
        image_own_body, (half, camera), [VM] * 4, (VM, VM), size, 2 * size, count * height
    )(before_own, rate, entry_intensity, emit)
    other_entered, part = call(
        image_other_body, (half, camera), [VM] * 5, (VM, VM), size, 2 * size, count * height
    )(before_other, rate, entry_intensity, emit, part)

    over_y = part
    for k in (1, 2, 3):
        over_y = over_y + lax.ppermute(part, "y", xor(4, k))
    sums = [over_y] + [lax.ppermute(over_y, "zl", xor(4, k)) for k in (3, 2, 1)]

    def adjoint_other(*refs):
        adjoint_other_body(scale, *refs)

    full_residual, back, other = call(
        adjoint_other, (camera, camera, half), [VM] * 4 + [SM] + [VM] * 3, (VM,) * 3, size, 2 * size
    )(*sums, blur_taps, measured, emit, other_entered)
    partner = lax.ppermute(other, "core", xor(2, 1))
    own = call(adjoint_own_body, half, [VM] * 3, VM, size, 2 * size)(back, emit, own_entered)
    known, columns = call(
        partial_body, (blocks, jax.ShapeDtypeStruct((width, beam), F32)), [VM] * 7, (VM, VM),
        6 * size, 12 * size, scratch=(pltpu.VMEM((height, beam), F32),),
    )(rate, back, full_residual, own_entered, other_entered, light, emit)
    after_own, after_other = scanned(own, partner, flags, True)
    written_scratch = (pltpu.VMEM((beam, count, height), F32), copied)
    whole = jax.ShapeDtypeStruct((beam, depth, height), F32)
    begun = call(
        final_own_body, whole, [VM] * 3, HBM, size // 2, 6 * size, scratch=written_scratch
    )(after_own, rate, known)
    descent = call(
        final_other_body, whole, [VM] * 3 + [HBM], HBM, size // 2, 6 * size, scratch=written_scratch,
        aliases={3: 0},
    )(after_other, rate, known, begun)
    return descent, columns.T


def solution(mesh):
    finer = Mesh(mesh.devices.reshape(4, 2, 2, 4, 4), BEAM + DEPTH)
    placed = (P(BEAM, DEPTH, None), P(DEPTH, None), P(), P(), P(BEAM, None))
    return jax.shard_map(
        local,
        mesh=finer,
        in_specs=placed,
        out_specs=(P(BEAM, DEPTH, None), P(BEAM, DEPTH)),
        check_vma=False,
    )
```

time: 67.9 us -> 67.5 us (level)
  waiting for transfers between devices: 22 us -> 20.4 us
  Pallas kernels: 8.41 us -> 9.91 us
    pallas_call x6 -> x10, Pallas kernels: 8.41 us -> 9.91 us  [the longest x1 1.68 us: local(): call(partial_body, (blocks, jax.ShapeDtypeStruct((width, beam), F32)), [V...]
    ppermute x5, waiting for transfers between devices: 6.36 us -> 5.26 us  [the longest x3 4.56 us: local(): sums = [over_y] + [lax.ppermute(over_y, 'zl', xor(4, k)) for k in (3, 2, 1)]]
    ppermute x2, waiting for transfers between devices: 6.01 us -> 5.31 us  [scanned(): crossed = lax.ppermute(sent, 'zh', xor(2, 1))]
  transfers between devices with their start and end apart: 18 -> 18, of which waited for: 14 -> 12; matrix products, arithmetic and copies ran while one was open for 0% -> 0% of each run, Pallas kernels for 4% -> 9%
where the time goes in v1:
time: 67.5 us; the launch traced here: 67.4 us
  starting transfers between devices  36.1 us (53%)
  waiting for transfers between devices  20.4 us (30%)
  Pallas kernels  9.91 us (15%)
  between operations  0.79 us (1%)
    ppermute x2, starting transfers between devices, scanned(): crossed = lax.ppermute(sent, 'zh', xor(2, 1))  9.38 us
    ppermute x2, starting transfers between devices, local(): partner = lax.ppermute(other, 'core', xor(2, 1))  6.72 us
    ppermute x6, starting transfers between devices, scanned(): rows = [lax.ppermute(pair, 'x', xor(4, k)) for k in (1, 2, 3)]  6.68 us
    ppermute x6, waiting for transfers between devices, scanned(): rows = [lax.ppermute(pair, 'x', xor(4, k)) for k in (1, 2, 3)]  6.22 us
    ppermute x2, starting transfers between devices, scanned(): return (for_me, lax.ppermute(for_other, 'core', xor(2, 1)))  5.81 us
    ppermute x2, waiting for transfers between devices, scanned(): crossed = lax.ppermute(sent, 'zh', xor(2, 1))  5.31 us
    ppermute x3, waiting for transfers between devices, local(): sums = [over_y] + [lax.ppermute(over_y, 'zl', xor(4, k)) for k in (3, 2, 1)]  4.56 us
    ppermute x3, starting transfers between devices, local(): sums = [over_y] + [lax.ppermute(over_y, 'zl', xor(4, k)) for k in (3, 2, 1)]  4.05 us
  transfers between devices with their start and end apart: 18, of which 12 were waited for; matrix products, arithmetic and copies ran while one was open for 0% of the time, Pallas kernels for 9%

profile of v1, /device:TPU:1, one launch (start us, length us, event | category | flops | bytes accessed | tf_op | source)
XLA Modules:
  0.0 67.4 jit_solution(15822001218863263787)
XLA Ops:
  0.6 0.0 copy-start.1
  0.6 1.6 %shard_map.68 = (f32[32,64,256]{2,1,0:T(8,128)S(1)}, f32[64,256]{1,0:T(8,128)S(1)}, f32[8,256]{1,0:T(8,128)S(1)}) custom-call(f32[32,128,256]{2,1,0:T(8,128)} %c_hbm.3), custom_call_target="tpu_custom_call" | custom-call | flops 524288 | bytes 4194304 | tf_op jit(solution)/shard_map/pallas_call | solution.py:215
  2.2 0.0 copy-start
  2.3 3.3 %collective-permute-start = (f32[64,256]{1,0:T(8,128)S(1)}, f32[64,256]{1,0:T(8,128)S(1)}, u32[]{:S(2)}, u32[]{:S(2)}) collective-permute-start(f32[64,256]{1,0:T(8,128)S(1)} %get-tuple-element.20), channel_id=1, source_target_pairs={{0,16},{16,0},{1,17},{17,1},{2,18},{18,2},{3,19},{19,3},{4,20},{20... | collective-permute-start | bytes 196616 | tf_op jit(solution)/shard_map/ppermute | solution.py:219
  5.5 1.6 %shard_map.69 = (f32[32,64,256]{2,1,0:T(8,128)S(1)}, f32[64,256]{1,0:T(8,128)S(1)}) custom-call(f32[32,128,256]{2,1,0:T(8,128)} %c_hbm.3), custom_call_target="tpu_custom_call" | custom-call | flops 524288 | bytes 4194304 | tf_op jit(solution)/shard_map/pallas_call | solution.py:220
  7.1 0.0 collective-permute-done
  7.2 0.9 %collective-permute-start.3 = (f32[64,256]{1,0:T(8,128)S(1)}, f32[64,256]{1,0:T(8,128)S(1)}, u32[]{:S(2)}, u32[]{:S(2)}) collective-permute-start(f32[64,256]{1,0:T(8,128)S(1)} %add.51), channel_id=1, source_target_pairs={{0,192},{64,128},{128,64},{192,0},{1,193},{65,129},{129,65},{193,1... | collective-permute-start | bytes 196616 | tf_op jit(solution)/shard_map/ppermute | solution.py:190
  8.0 0.5 collective-permute-start.2
  8.5 2.0 %collective-permute-start.1 = (f32[64,256]{1,0:T(8,128)S(1)}, f32[64,256]{1,0:T(8,128)S(1)}, u32[]{:S(2)}, u32[]{:S(2)}) collective-permute-start(f32[64,256]{1,0:T(8,128)S(1)} %add.51), channel_id=1, source_target_pairs={{0,64},{64,0},{128,192},{192,128},{1,65},{65,1},{129,193},{193,129... | collective-permute-start | bytes 196616 | tf_op jit(solution)/shard_map/ppermute | solution.py:190
  10.5 1.6 %collective-permute-done.3 = f32[64,256]{1,0:T(8,128)S(1)} collective-permute-done((f32[64,256]{1,0:T(8,128)S(1)}, f32[64,256]{1,0:T(8,128)S(1)}, u32[]{:S(2)}, u32[]{:S(2)}) %collective-permute-start.3) | collective-permute-done | bytes 65568 | tf_op jit(solution)/shard_map/ppermute | solution.py:190
  12.1 0.7 collective-permute-done.2
  12.8 1.0 %collective-permute-done.1 = f32[64,256]{1,0:T(8,128)S(1)} collective-permute-done((f32[64,256]{1,0:T(8,128)S(1)}, f32[64,256]{1,0:T(8,128)S(1)}, u32[]{:S(2)}, u32[]{:S(2)}) %collective-permute-start.1) | collective-permute-done | bytes 65568 | tf_op jit(solution)/shard_map/ppermute | solution.py:190
  13.8 5.9 %collective-permute-start.4 = (f32[64,256]{1,0:T(8,128)S(1)}, f32[64,256]{1,0:T(8,128)S(1)}, u32[]{:S(2)}, u32[]{:S(2)}) collective-permute-start(f32[64,256]{1,0:T(8,128)S(1)} %get-tuple-element.36), channel_id=1, source_target_pairs={{0,32},{32,0},{1,33},{33,1},{2,34},{34,2},{3,35},{35,3},{4,36},{36... | collective-permute-start | bytes 196616 | tf_op jit(solution)/shard_map/ppermute | solution.py:193
  19.7 1.7 %collective-permute-done.4 = f32[64,256]{1,0:T(8,128)S(1)} collective-permute-done((f32[64,256]{1,0:T(8,128)S(1)}, f32[64,256]{1,0:T(8,128)S(1)}, u32[]{:S(2)}, u32[]{:S(2)}) %collective-permute-start.4) | collective-permute-done | bytes 65568 | tf_op jit(solution)/shard_map/ppermute | solution.py:193
  21.4 3.1 %collective-permute-start.5 = (f32[64,256]{1,0:T(8,128)S(1)}, f32[64,256]{1,0:T(8,128)S(1)}, u32[]{:S(2)}, u32[]{:S(2)}) collective-permute-start(f32[64,256]{1,0:T(8,128)S(1)} %get-tuple-element.41), channel_id=1, source_target_pairs={{0,16},{16,0},{1,17},{17,1},{2,18},{18,2},{3,19},{19,3},{4,20},{20... | collective-permute-start | bytes 196616 | tf_op jit(solution)/shard_map/ppermute | solution.py:197
  24.5 0.0 copy-done.1
  24.5 0.8 %shard_map.70 = (f32[2,32,64,256]{3,2,1,0:T(8,128)S(1)}, f32[2,32,64,256]{3,2,1,0:T(8,128)S(1)}) custom-call(f32[32,64,256]{2,1,0:T(8,128)S(1)} %get-tuple-element.21.own_ref, f32[32,64,256]{2,1,0:T(8,128)S(1)} %get-tuple-element.22.other_ref, f32[1,256]{1,0:T(1,128)S(1)} %bitcast.14), custom_call_target="tpu_custom_call" | custom-call | flops 4194304 | bytes 12582912 | tf_op jit(solution)/shard_map/pallas_call | solution.py:223
  25.3 0.0 copy-done
  25.3 0.0 copy-start.2
  25.3 0.0 copy-start.3
  25.3 0.2 shard_map.71
  25.5 0.0 collective-permute-done.5.before_ref
  25.5 0.2 shard_map.72
  25.8 2.8 %collective-permute-start.8 = (f32[32,256]{1,0:T(8,128)S(1)}, f32[32,256]{1,0:T(8,128)S(1)}, u32[]{:S(2)}, u32[]{:S(2)}) collective-permute-start(f32[32,256]{1,0:T(8,128)S(1)} %get-tuple-element.25), channel_id=1, source_target_pairs={{0,12},{4,8},{8,4},{12,0},{1,13},{5,9},{9,5},{13,1},{2,14},{6,10},... | collective-permute-start | bytes 98312 | tf_op jit(solution)/shard_map/ppermute | solution.py:236
  28.6 0.3 collective-permute-start.7
  29.0 0.3 collective-permute-start.6
  29.3 0.6 collective-permute-done.8
  29.9 3.0 %collective-permute-done.7 = f32[32,256]{1,0:T(8,128)S(1)} collective-permute-done((f32[32,256]{1,0:T(8,128)S(1)}, f32[32,256]{1,0:T(8,128)S(1)}, u32[]{:S(2)}, u32[]{:S(2)}) %collective-permute-start.7) | collective-permute-done | bytes 32800 | tf_op jit(solution)/shard_map/ppermute | solution.py:236
  32.9 0.0 collective-permute-done.6
  32.9 1.2 %collective-permute-start.11 = (f32[32,256]{1,0:T(8,128)S(1)}, f32[32,256]{1,0:T(8,128)S(1)}, u32[]{:S(2)}, u32[]{:S(2)}) collective-permute-start(f32[32,256]{1,0:T(8,128)S(1)} %add_add_fusion.refs_0_), channel_id=1, source_target_pairs={{0,1},{1,0},{2,3},{3,2},{4,5},{5,4},{6,7},{7,6},{8,9},{9,8},{10,11... | collective-permute-start | bytes 98312 | tf_op jit(solution)/shard_map/ppermute | solution.py:237
  34.1 2.8 %collective-permute-start.10 = (f32[32,256]{1,0:T(8,128)S(1)}, f32[32,256]{1,0:T(8,128)S(1)}, u32[]{:S(2)}, u32[]{:S(2)}) collective-permute-start(f32[32,256]{1,0:T(8,128)S(1)} %add_add_fusion.refs_0_), channel_id=1, source_target_pairs={{0,2},{1,3},{2,0},{3,1},{4,6},{5,7},{6,4},{7,5},{8,10},{9,11},{10,... | collective-permute-start | bytes 98312 | tf_op jit(solution)/shard_map/ppermute | solution.py:237
  36.9 0.0 collective-permute-start.9
  36.9 0.0 collective-permute-done.11.refs_3_
  36.9 1.6 %collective-permute-done.10.refs_2_ = f32[32,256]{1,0:T(8,128)S(1)} collective-permute-done((f32[32,256]{1,0:T(8,128)S(1)}, f32[32,256]{1,0:T(8,128)S(1)}, u32[]{:S(2)}, u32[]{:S(2)}) %collective-permute-start.10) | collective-permute-done | bytes 32800 | tf_op jit(solution)/shard_map/ppermute | solution.py:237
  38.6 2.9 %collective-permute-done.9.refs_1_ = f32[32,256]{1,0:T(8,128)S(1)} collective-permute-done((f32[32,256]{1,0:T(8,128)S(1)}, f32[32,256]{1,0:T(8,128)S(1)}, u32[]{:S(2)}, u32[]{:S(2)}) %collective-permute-start.9) | collective-permute-done | bytes 32800 | tf_op jit(solution)/shard_map/ppermute | solution.py:237
  41.5 0.0 copy-done.2
  41.5 0.0 copy-done.3
  41.5 0.9 %shard_map.73 = (f32[32,256]{1,0:T(8,128)S(1)}, f32[32,256]{1,0:T(8,128)S(1)}, f32[64,256]{1,0:T(8,128)S(1)}) custom-call(f32[32,256]{1,0:T(8,128)S(1)} %add_add_fusion.refs_0_, f32[32,256]{1,0:T(8,128)S(1)} %collective-permute-done.9.refs_1_, f32[32,256]{1,0:T(8,128)S(1)} %collective-permute-done.10.refs_2_, f32[32,256]{1,0:T(8,128)S(1)} %collective-permute-done.11.refs_3_, ...), custom_call_target="tpu_custom_call" | custom-call | flops 1048576 | bytes 2097152 | tf_op jit(solution)/shard_map/pallas_call | solution.py:242
  42.4 3.4 %collective-permute-start.12 = (f32[64,256]{1,0:T(8,128)S(1)}, f32[64,256]{1,0:T(8,128)S(1)}, u32[]{:S(2)}, u32[]{:S(2)}) collective-permute-start(f32[64,256]{1,0:T(8,128)S(1)} %get-tuple-element.29), channel_id=1, source_target_pairs={{0,16},{16,0},{1,17},{17,1},{2,18},{18,2},{3,19},{19,3},{4,20},{20... | collective-permute-start | bytes 196616 | tf_op jit(solution)/shard_map/ppermute | solution.py:245
  45.8 0.2 shard_map.74
  46.0 0.7 %collective-permute-done.12 = f32[64,256]{1,0:T(8,128)S(1)} collective-permute-done((f32[64,256]{1,0:T(8,128)S(1)}, f32[64,256]{1,0:T(8,128)S(1)}, u32[]{:S(2)}, u32[]{:S(2)}) %collective-permute-start.12) | collective-permute-done | bytes 65568 | tf_op jit(solution)/shard_map/ppermute | solution.py:245
  46.7 0.4 collective-permute-start.15
  47.1 0.7 collective-permute-start.14
  47.7 2.3 %collective-permute-start.13 = (f32[64,256]{1,0:T(8,128)S(1)}, f32[64,256]{1,0:T(8,128)S(1)}, u32[]{:S(2)}, u32[]{:S(2)}) collective-permute-start(f32[64,256]{1,0:T(8,128)S(1)} %add.61), channel_id=1, source_target_pairs={{0,64},{64,0},{128,192},{192,128},{1,65},{65,1},{129,193},{193,129... | collective-permute-start | bytes 196616 | tf_op jit(solution)/shard_map/ppermute | solution.py:190
  50.1 2.1 %collective-permute-done.15 = f32[64,256]{1,0:T(8,128)S(1)} collective-permute-done((f32[64,256]{1,0:T(8,128)S(1)}, f32[64,256]{1,0:T(8,128)S(1)}, u32[]{:S(2)}, u32[]{:S(2)}) %collective-permute-start.15) | collective-permute-done | bytes 65568 | tf_op jit(solution)/shard_map/ppermute | solution.py:190
  52.2 0.0 collective-permute-done.14
  52.2 0.9 %collective-permute-done.13 = f32[64,256]{1,0:T(8,128)S(1)} collective-permute-done((f32[64,256]{1,0:T(8,128)S(1)}, f32[64,256]{1,0:T(8,128)S(1)}, u32[]{:S(2)}, u32[]{:S(2)}) %collective-permute-start.13) | collective-permute-done | bytes 65568 | tf_op jit(solution)/shard_map/ppermute | solution.py:190
  53.0 3.5 %collective-permute-start.16 = (f32[64,256]{1,0:T(8,128)S(1)}, f32[64,256]{1,0:T(8,128)S(1)}, u32[]{:S(2)}, u32[]{:S(2)}) collective-permute-start(f32[64,256]{1,0:T(8,128)S(1)} %get-tuple-element.34), channel_id=1, source_target_pairs={{0,32},{32,0},{1,33},{33,1},{2,34},{34,2},{3,35},{35,3},{4,36},{36... | collective-permute-start | bytes 196616 | tf_op jit(solution)/shard_map/ppermute | solution.py:193
  56.6 3.6 %collective-permute-done.16 = f32[64,256]{1,0:T(8,128)S(1)} collective-permute-done((f32[64,256]{1,0:T(8,128)S(1)}, f32[64,256]{1,0:T(8,128)S(1)}, u32[]{:S(2)}, u32[]{:S(2)}) %collective-permute-start.16) | collective-permute-done | bytes 65568 | tf_op jit(solution)/shard_map/ppermute | solution.py:193
  60.2 2.7 %collective-permute-start.17 = (f32[64,256]{1,0:T(8,128)S(1)}, f32[64,256]{1,0:T(8,128)S(1)}, u32[]{:S(2)}, u32[]{:S(2)}) collective-permute-start(f32[64,256]{1,0:T(8,128)S(1)} %get-tuple-element.39), channel_id=1, source_target_pairs={{0,16},{16,0},{1,17},{17,1},{2,18},{18,2},{3,19},{19,3},{4,20},{20... | collective-permute-start | bytes 196616 | tf_op jit(solution)/shard_map/ppermute | solution.py:197
  62.9 1.7 %shard_map.75 = (f32[2,32,64,256]{3,2,1,0:T(8,128)S(1)}, f32[16,32]{1,0:T(8,128)}) custom-call(f32[1,256]{1,0:T(1,128)S(1)} %bitcast.17, f32[32,256]{1,0:T(8,128)S(1)} %get-tuple-element.27.back_ref, f32[32,256]{1,0:T(8,128)S(1)} %get-tuple-element.30.residual_ref, f32[64,256]{1,0:T(8,128)S(1)} %get-tuple-element.28.entered_ref.own_entered_ref, ...), custom_call_target="tpu_custom_call" | custom-call | flops 6291456 | bytes 12582912 | tf_op jit(solution)/shard_map/pallas_call | solution.py:247
  64.6 1.4 %shard_map.76.begun_hbm = f32[32,128,256]{2,1,0:T(8,128)} custom-call(f32[64,256]{1,0:T(8,128)S(1)} %get-tuple-element.38.after_ref, f32[1,256]{1,0:T(1,128)S(1)} %bitcast.18, f32[2,32,64,256]{3,2,1,0:T(8,128)S(1)} %get-tuple-element.32.known_ref), custom_call_target="tpu_custom_call" | custom-call | flops 524288 | bytes 6291456 | tf_op jit(solution)/shard_map/pallas_call | solution.py:254
  66.0 0.0 collective-permute-done.17.after_ref
  66.0 1.4 %shard_map.77 = f32[32,128,256]{2,1,0:T(8,128)} custom-call(f32[64,256]{1,0:T(8,128)S(1)} %collective-permute-done.17.after_ref, f32[1,256]{1,0:T(1,128)S(1)} %bitcast.19, f32[2,32,64,256]{3,2,1,0:T(8,128)S(1)} %get-tuple-element.32.known_ref, f32[32,128,256]{2,1,0:T(8,128)} %shard_map.76.begun_hbm), custom_call_target="tpu_custom_call", output_to_operand_aliasing={{}: (3, {})} | custom-call | flops 524288 | bytes 6291456 | tf_op jit(solution)/shard_map/pallas_call | solution.py:257
  (10 shorter events, 0.1 us)
Async XLA Ops:
  0.6 23.9 %copy-start.1 = (f32[256]{0:T(256)S(1)}, f32[256]{0:T(256)}, u32[]{:S(2)}) copy-start(f32[256]{0:T(256)} %param.7) | copy-start | bytes 3076
  2.2 23.0 %copy-start = (f32[128,256]{1,0:T(8,128)S(1)}, f32[128,256]{1,0:T(8,128)}, u32[]{:S(2)}) copy-start(f32[128,256]{1,0:T(8,128)} %entry_ref.3) | copy-start | bytes 393220
  2.3 4.9 %collective-permute-start = (f32[64,256]{1,0:T(8,128)S(1)}, f32[64,256]{1,0:T(8,128)S(1)}, u32[]{:S(2)}, u32[]{:S(2)}) collective-permute-start(f32[64,256]{1,0:T(8,128)S(1)} %get-tuple-element.20), channel_id=1, source_target_pairs={{0,16},{16,0},{1,17},{17,1},{2,18},{18,2},{3,19},{19,3},{4,20},{20... | collective-permute-start | bytes 196616 | tf_op jit(solution)/shard_map/ppermute | solution.py:219
  7.2 4.9 %collective-permute-start.3 = (f32[64,256]{1,0:T(8,128)S(1)}, f32[64,256]{1,0:T(8,128)S(1)}, u32[]{:S(2)}, u32[]{:S(2)}) collective-permute-start(f32[64,256]{1,0:T(8,128)S(1)} %add.51), channel_id=1, source_target_pairs={{0,192},{64,128},{128,64},{192,0},{1,193},{65,129},{129,65},{193,1... | collective-permute-start | bytes 196616 | tf_op jit(solution)/shard_map/ppermute | solution.py:190
  8.0 4.7 %collective-permute-start.2 = (f32[64,256]{1,0:T(8,128)S(1)}, f32[64,256]{1,0:T(8,128)S(1)}, u32[]{:S(2)}, u32[]{:S(2)}) collective-permute-start(f32[64,256]{1,0:T(8,128)S(1)} %add.51), channel_id=1, source_target_pairs={{0,128},{64,192},{128,0},{192,64},{1,129},{65,193},{129,1},{193,65... | collective-permute-start | bytes 196616 | tf_op jit(solution)/shard_map/ppermute | solution.py:190
  8.5 5.2 %collective-permute-start.1 = (f32[64,256]{1,0:T(8,128)S(1)}, f32[64,256]{1,0:T(8,128)S(1)}, u32[]{:S(2)}, u32[]{:S(2)}) collective-permute-start(f32[64,256]{1,0:T(8,128)S(1)} %add.51), channel_id=1, source_target_pairs={{0,64},{64,0},{128,192},{192,128},{1,65},{65,1},{129,193},{193,129... | collective-permute-start | bytes 196616 | tf_op jit(solution)/shard_map/ppermute | solution.py:190
  13.8 7.6 %collective-permute-start.4 = (f32[64,256]{1,0:T(8,128)S(1)}, f32[64,256]{1,0:T(8,128)S(1)}, u32[]{:S(2)}, u32[]{:S(2)}) collective-permute-start(f32[64,256]{1,0:T(8,128)S(1)} %get-tuple-element.36), channel_id=1, source_target_pairs={{0,32},{32,0},{1,33},{33,1},{2,34},{34,2},{3,35},{35,3},{4,36},{36... | collective-permute-start | bytes 196616 | tf_op jit(solution)/shard_map/ppermute | solution.py:193
  21.4 4.1 %collective-permute-start.5 = (f32[64,256]{1,0:T(8,128)S(1)}, f32[64,256]{1,0:T(8,128)S(1)}, u32[]{:S(2)}, u32[]{:S(2)}) collective-permute-start(f32[64,256]{1,0:T(8,128)S(1)} %get-tuple-element.41), channel_id=1, source_target_pairs={{0,16},{16,0},{1,17},{17,1},{2,18},{18,2},{3,19},{19,3},{4,20},{20... | collective-permute-start | bytes 196616 | tf_op jit(solution)/shard_map/ppermute | solution.py:197
  25.3 16.2 %copy-start.2 = (f32[32,256]{1,0:T(8,128)S(1)}, f32[32,256]{1,0:T(8,128)}, u32[]{:S(2)}) copy-start(f32[32,256]{1,0:T(8,128)} %refs_5_.1) | copy-start | bytes 98308
  25.3 16.2 %copy-start.3 = (f32[5]{0:T(128)S(1)}, f32[5]{0:T(128)}, u32[]{:S(2)}) copy-start(f32[5]{0:T(128)} %refs_4_.1) | copy-start | bytes 64
  25.8 4.1 %collective-permute-start.8 = (f32[32,256]{1,0:T(8,128)S(1)}, f32[32,256]{1,0:T(8,128)S(1)}, u32[]{:S(2)}, u32[]{:S(2)}) collective-permute-start(f32[32,256]{1,0:T(8,128)S(1)} %get-tuple-element.25), channel_id=1, source_target_pairs={{0,12},{4,8},{8,4},{12,0},{1,13},{5,9},{9,5},{13,1},{2,14},{6,10},... | collective-permute-start | bytes 98312 | tf_op jit(solution)/shard_map/ppermute | solution.py:236
  28.6 4.3 %collective-permute-start.7 = (f32[32,256]{1,0:T(8,128)S(1)}, f32[32,256]{1,0:T(8,128)S(1)}, u32[]{:S(2)}, u32[]{:S(2)}) collective-permute-start(f32[32,256]{1,0:T(8,128)S(1)} %get-tuple-element.25), channel_id=1, source_target_pairs={{0,8},{4,12},{8,0},{12,4},{1,9},{5,13},{9,1},{13,5},{2,10},{6,14},... | collective-permute-start | bytes 98312 | tf_op jit(solution)/shard_map/ppermute | solution.py:236
  29.0 3.9 %collective-permute-start.6 = (f32[32,256]{1,0:T(8,128)S(1)}, f32[32,256]{1,0:T(8,128)S(1)}, u32[]{:S(2)}, u32[]{:S(2)}) collective-permute-start(f32[32,256]{1,0:T(8,128)S(1)} %get-tuple-element.25), channel_id=1, source_target_pairs={{0,4},{4,0},{8,12},{12,8},{1,5},{5,1},{9,13},{13,9},{2,6},{6,2},{1... | collective-permute-start | bytes 98312 | tf_op jit(solution)/shard_map/ppermute | solution.py:236
  32.9 4.1 %collective-permute-start.11 = (f32[32,256]{1,0:T(8,128)S(1)}, f32[32,256]{1,0:T(8,128)S(1)}, u32[]{:S(2)}, u32[]{:S(2)}) collective-permute-start(f32[32,256]{1,0:T(8,128)S(1)} %add_add_fusion.refs_0_), channel_id=1, source_target_pairs={{0,1},{1,0},{2,3},{3,2},{4,5},{5,4},{6,7},{7,6},{8,9},{9,8},{10,11... | collective-permute-start | bytes 98312 | tf_op jit(solution)/shard_map/ppermute | solution.py:237
  34.1 4.5 %collective-permute-start.10 = (f32[32,256]{1,0:T(8,128)S(1)}, f32[32,256]{1,0:T(8,128)S(1)}, u32[]{:S(2)}, u32[]{:S(2)}) collective-permute-start(f32[32,256]{1,0:T(8,128)S(1)} %add_add_fusion.refs_0_), channel_id=1, source_target_pairs={{0,2},{1,3},{2,0},{3,1},{4,6},{5,7},{6,4},{7,5},{8,10},{9,11},{10,... | collective-permute-start | bytes 98312 | tf_op jit(solution)/shard_map/ppermute | solution.py:237
  36.9 4.6 %collective-permute-start.9 = (f32[32,256]{1,0:T(8,128)S(1)}, f32[32,256]{1,0:T(8,128)S(1)}, u32[]{:S(2)}, u32[]{:S(2)}) collective-permute-start(f32[32,256]{1,0:T(8,128)S(1)} %add_add_fusion.refs_0_), channel_id=1, source_target_pairs={{0,3},{1,2},{2,1},{3,0},{4,7},{5,6},{6,5},{7,4},{8,11},{9,10},{10,... | collective-permute-start | bytes 98312 | tf_op jit(solution)/shard_map/ppermute | solution.py:237
  42.4 4.3 %collective-permute-start.12 = (f32[64,256]{1,0:T(8,128)S(1)}, f32[64,256]{1,0:T(8,128)S(1)}, u32[]{:S(2)}, u32[]{:S(2)}) collective-permute-start(f32[64,256]{1,0:T(8,128)S(1)} %get-tuple-element.29), channel_id=1, source_target_pairs={{0,16},{16,0},{1,17},{17,1},{2,18},{18,2},{3,19},{19,3},{4,20},{20... | collective-permute-start | bytes 196616 | tf_op jit(solution)/shard_map/ppermute | solution.py:245
  46.7 5.4 %collective-permute-start.15 = (f32[64,256]{1,0:T(8,128)S(1)}, f32[64,256]{1,0:T(8,128)S(1)}, u32[]{:S(2)}, u32[]{:S(2)}) collective-permute-start(f32[64,256]{1,0:T(8,128)S(1)} %add.61), channel_id=1, source_target_pairs={{0,192},{64,128},{128,64},{192,0},{1,193},{65,129},{129,65},{193,1... | collective-permute-start | bytes 196616 | tf_op jit(solution)/shard_map/ppermute | solution.py:190
  47.1 5.1 %collective-permute-start.14 = (f32[64,256]{1,0:T(8,128)S(1)}, f32[64,256]{1,0:T(8,128)S(1)}, u32[]{:S(2)}, u32[]{:S(2)}) collective-permute-start(f32[64,256]{1,0:T(8,128)S(1)} %add.61), channel_id=1, source_target_pairs={{0,128},{64,192},{128,0},{192,64},{1,129},{65,193},{129,1},{193,65... | collective-permute-start | bytes 196616 | tf_op jit(solution)/shard_map/ppermute | solution.py:190
  47.7 5.3 %collective-permute-start.13 = (f32[64,256]{1,0:T(8,128)S(1)}, f32[64,256]{1,0:T(8,128)S(1)}, u32[]{:S(2)}, u32[]{:S(2)}) collective-permute-start(f32[64,256]{1,0:T(8,128)S(1)} %add.61), channel_id=1, source_target_pairs={{0,64},{64,0},{128,192},{192,128},{1,65},{65,1},{129,193},{193,129... | collective-permute-start | bytes 196616 | tf_op jit(solution)/shard_map/ppermute | solution.py:190
  53.0 7.1 %collective-permute-start.16 = (f32[64,256]{1,0:T(8,128)S(1)}, f32[64,256]{1,0:T(8,128)S(1)}, u32[]{:S(2)}, u32[]{:S(2)}) collective-permute-start(f32[64,256]{1,0:T(8,128)S(1)} %get-tuple-element.34), channel_id=1, source_target_pairs={{0,32},{32,0},{1,33},{33,1},{2,34},{34,2},{3,35},{35,3},{4,36},{36... | collective-permute-start | bytes 196616 | tf_op jit(solution)/shard_map/ppermute | solution.py:193
  60.2 5.8 %collective-permute-start.17 = (f32[64,256]{1,0:T(8,128)S(1)}, f32[64,256]{1,0:T(8,128)S(1)}, u32[]{:S(2)}, u32[]{:S(2)}) collective-permute-start(f32[64,256]{1,0:T(8,128)S(1)} %get-tuple-element.39), channel_id=1, source_target_pairs={{0,16},{16,0},{1,17},{17,1},{2,18},{18,2},{3,19},{19,3},{4,20},{20... | collective-permute-start | bytes 196616 | tf_op jit(solution)/shard_map/ppermute | solution.py:197

commit v2 on v1

--- a/solution.py
+++ b/solution.py
@@ -136,13 +136,15 @@
     total_ref[...] = weighed(0, back_ref, emit_ref, entered_ref)
 
 
-def partial_body(absorb_ref, back_ref, residual_ref, own_entered_ref, other_entered_ref, light_ref, emit_ref,
-                 known_ref, columns_ref, turned_ref):
-    _, beam, count, height = light_ref.shape
+def turn_body(residual_ref, columns_ref, turned_ref):
     width = columns_ref.shape[0]
     section = (lax.axis_index("y") * lax.axis_size("zl") + lax.axis_index("zl")) * width
     turned_ref[...] = residual_ref[...].T
     columns_ref[...] = turned_ref[pl.ds(pl.multiple_of(section, 8), width), :]
+
+
+def partial_body(absorb_ref, back_ref, own_entered_ref, other_entered_ref, light_ref, emit_ref, known_ref):
+    _, beam, count, height = light_ref.shape
     absorb = jnp.broadcast_to(absorb_ref[...], (8, height))
     for half, entered_ref in enumerate((own_entered_ref, other_entered_ref)):
 
@@ -187,11 +189,10 @@
         flags = 1.0 - flags
     late_z, late_core = flags[0:1], flags[1:2]
     pair = own + partner
-    rows = [lax.ppermute(pair, "x", xor(4, k)) for k in (1, 2, 3)]
-    over_x = flags[2:3] * rows[0] + flags[3:4] * rows[1] + flags[4:5] * rows[2]
-    sent = over_x + (1.0 - late_z) * pair
-    crossed = lax.ppermute(sent, "zh", xor(2, 1))
-    base = over_x + crossed
+    crossed = lax.ppermute(pair, "zh", xor(2, 1))
+    both = pair + crossed
+    rows = [lax.ppermute(both, "x", xor(4, k)) for k in (1, 2, 3)]
+    base = flags[2:3] * rows[0] + flags[3:4] * rows[1] + flags[4:5] * rows[2] + late_z * crossed
     for_me = base + late_core * partner
     for_other = base + (1.0 - late_core) * own
     return for_me, lax.ppermute(for_other, "core", xor(2, 1))
@@ -231,10 +232,10 @@
         image_other_body, (half, camera), [VM] * 5, (VM, VM), size, 2 * size, count * height
     )(before_other, rate, entry_intensity, emit, part)
 
-    over_y = part
+    over_z = part
     for k in (1, 2, 3):
-        over_y = over_y + lax.ppermute(part, "y", xor(4, k))
-    sums = [over_y] + [lax.ppermute(over_y, "zl", xor(4, k)) for k in (3, 2, 1)]
+        over_z = over_z + lax.ppermute(part, "zl", xor(4, k))
+    sums = [over_z] + [lax.ppermute(over_z, "y", xor(4, k)) for k in (1, 2, 3)]
 
     def adjoint_other(*refs):
         adjoint_other_body(scale, *refs)
@@ -244,10 +245,13 @@
     )(*sums, blur_taps, measured, emit, other_entered)
     partner = lax.ppermute(other, "core", xor(2, 1))
     own = call(adjoint_own_body, half, [VM] * 3, VM, size, 2 * size)(back, emit, own_entered)
-    known, columns = call(
-        partial_body, (blocks, jax.ShapeDtypeStruct((width, beam), F32)), [VM] * 7, (VM, VM),
-        6 * size, 12 * size, scratch=(pltpu.VMEM((height, beam), F32),),
-    )(rate, back, full_residual, own_entered, other_entered, light, emit)
+    known = call(partial_body, blocks, [VM] * 6, VM, 6 * size, 12 * size)(
+        rate, back, own_entered, other_entered, light, emit
+    )
+    columns = call(
+        turn_body, jax.ShapeDtypeStruct((width, beam), F32), [VM], VM, 32768, 65536,
+        scratch=(pltpu.VMEM((height, beam), F32),),
+    )(full_residual)
     after_own, after_other = scanned(own, partner, flags, True)
     written_scratch = (pltpu.VMEM((beam, count, height), F32), copied)
     whole = jax.ShapeDtypeStruct((beam, depth, height), F32)

time: 67.5 us -> 65 us (0.963)
  the two profiles are of different devices: /device:TPU:1 before, /device:TPU:65 now
where the time goes in v2:
time: 65 us; the launch traced here: 64 us
  starting transfers between devices  31.6 us (49%)
  waiting for transfers between devices  21.5 us (33%)
  Pallas kernels  9.93 us (15%)
  between operations  0.81 us (1%)
    ppermute x2, starting transfers between devices, scanned(): crossed = lax.ppermute(pair, 'zh', xor(2, 1))  9.82 us
    ppermute x2, waiting for transfers between devices, scanned(): crossed = lax.ppermute(pair, 'zh', xor(2, 1))  8.11 us
    ppermute x6, starting transfers between devices, scanned(): rows = [lax.ppermute(both, 'x', xor(4, k)) for k in (1, 2, 3)]  6.68 us
    ppermute x6, waiting for transfers between devices, scanned(): rows = [lax.ppermute(both, 'x', xor(4, k)) for k in (1, 2, 3)]  6.48 us
    ppermute x2, starting transfers between devices, scanned(): return (for_me, lax.ppermute(for_other, 'core', xor(2, 1)))  5 us
    ppermute x2, starting transfers between devices, local(): partner = lax.ppermute(other, 'core', xor(2, 1))  3.87 us
    ppermute x3, waiting for transfers between devices, local(): sums = [over_z] + [lax.ppermute(over_z, 'y', xor(4, k)) for k in (1, 2, 3)]  3.59 us
    ppermute x3, starting transfers between devices, local(): sums = [over_z] + [lax.ppermute(over_z, 'y', xor(4, k)) for k in (1, 2, 3)]  3.5 us
  transfers between devices with their start and end apart: 18, of which 13 were waited for; matrix products, arithmetic and copies ran while one was open for 0% of the time, Pallas kernels for 9%

profile of v2, /device:TPU:65, one launch (start us, length us, event | category | flops | bytes accessed | tf_op | source)
XLA Modules:
  0.0 64.0 jit_solution(14225275908335270780)
XLA Ops:
  0.6 0.0 copy-start.1
  0.6 1.6 %shard_map.68 = (f32[32,64,256]{2,1,0:T(8,128)S(1)}, f32[64,256]{1,0:T(8,128)S(1)}, f32[8,256]{1,0:T(8,128)S(1)}) custom-call(f32[32,128,256]{2,1,0:T(8,128)} %c_hbm.3), custom_call_target="tpu_custom_call" | custom-call | flops 524288 | bytes 4194304 | tf_op jit(solution)/shard_map/pallas_call | solution.py:216
  2.2 0.0 copy-start
  2.3 0.8 %collective-permute-start = (f32[64,256]{1,0:T(8,128)S(1)}, f32[64,256]{1,0:T(8,128)S(1)}, u32[]{:S(2)}, u32[]{:S(2)}) collective-permute-start(f32[64,256]{1,0:T(8,128)S(1)} %get-tuple-element.18), channel_id=1, source_target_pairs={{0,16},{16,0},{1,17},{17,1},{2,18},{18,2},{3,19},{19,3},{4,20},{20... | collective-permute-start | bytes 196616 | tf_op jit(solution)/shard_map/ppermute | solution.py:220
  3.0 1.6 %shard_map.69 = (f32[32,64,256]{2,1,0:T(8,128)S(1)}, f32[64,256]{1,0:T(8,128)S(1)}) custom-call(f32[32,128,256]{2,1,0:T(8,128)} %c_hbm.3), custom_call_target="tpu_custom_call" | custom-call | flops 524288 | bytes 4194304 | tf_op jit(solution)/shard_map/pallas_call | solution.py:221
  4.6 0.0 collective-permute-done
  4.6 5.2 %collective-permute-start.1 = (f32[64,256]{1,0:T(8,128)S(1)}, f32[64,256]{1,0:T(8,128)S(1)}, u32[]{:S(2)}, u32[]{:S(2)}) collective-permute-start(f32[64,256]{1,0:T(8,128)S(1)} %add.51), channel_id=1, source_target_pairs={{0,32},{32,0},{1,33},{33,1},{2,34},{34,2},{3,35},{35,3},{4,36},{36... | collective-permute-start | bytes 196616 | tf_op jit(solution)/shard_map/ppermute | solution.py:192
  9.8 3.8 %collective-permute-done.1 = f32[64,256]{1,0:T(8,128)S(1)} collective-permute-done((f32[64,256]{1,0:T(8,128)S(1)}, f32[64,256]{1,0:T(8,128)S(1)}, u32[]{:S(2)}, u32[]{:S(2)}) %collective-permute-start.1) | collective-permute-done | bytes 65568 | tf_op jit(solution)/shard_map/ppermute | solution.py:192
  13.7 2.6 %collective-permute-start.4 = (f32[64,256]{1,0:T(8,128)S(1)}, f32[64,256]{1,0:T(8,128)S(1)}, u32[]{:S(2)}, u32[]{:S(2)}) collective-permute-start(f32[64,256]{1,0:T(8,128)S(1)} %add.52), channel_id=1, source_target_pairs={{0,192},{64,128},{128,64},{192,0},{1,193},{65,129},{129,65},{193,1... | collective-permute-start | bytes 196616 | tf_op jit(solution)/shard_map/ppermute | solution.py:194
  16.2 0.5 collective-permute-start.3
  16.8 0.3 collective-permute-start.2
  17.0 1.1 %collective-permute-done.4 = f32[64,256]{1,0:T(8,128)S(1)} collective-permute-done((f32[64,256]{1,0:T(8,128)S(1)}, f32[64,256]{1,0:T(8,128)S(1)}, u32[]{:S(2)}, u32[]{:S(2)}) %collective-permute-start.4) | collective-permute-done | bytes 65568 | tf_op jit(solution)/shard_map/ppermute | solution.py:194
  18.1 2.8 %collective-permute-done.3 = f32[64,256]{1,0:T(8,128)S(1)} collective-permute-done((f32[64,256]{1,0:T(8,128)S(1)}, f32[64,256]{1,0:T(8,128)S(1)}, u32[]{:S(2)}, u32[]{:S(2)}) %collective-permute-start.3) | collective-permute-done | bytes 65568 | tf_op jit(solution)/shard_map/ppermute | solution.py:194
  20.9 0.0 collective-permute-done.2
  20.9 2.6 %collective-permute-start.5 = (f32[64,256]{1,0:T(8,128)S(1)}, f32[64,256]{1,0:T(8,128)S(1)}, u32[]{:S(2)}, u32[]{:S(2)}) collective-permute-start(f32[64,256]{1,0:T(8,128)S(1)} %multiply_add_fusion.4), channel_id=1, source_target_pairs={{0,16},{16,0},{1,17},{17,1},{2,18},{18,2},{3,19},{19,3},{4,20},{20... | collective-permute-start | bytes 196616 | tf_op jit(solution)/shard_map/ppermute | solution.py:198
  23.5 0.0 copy-done.1
  23.5 0.8 %shard_map.70 = (f32[2,32,64,256]{3,2,1,0:T(8,128)S(1)}, f32[2,32,64,256]{3,2,1,0:T(8,128)S(1)}) custom-call(f32[32,64,256]{2,1,0:T(8,128)S(1)} %get-tuple-element.19.own_ref, f32[32,64,256]{2,1,0:T(8,128)S(1)} %get-tuple-element.20.other_ref, f32[1,256]{1,0:T(1,128)S(1)} %bitcast.14), custom_call_target="tpu_custom_call" | custom-call | flops 4194304 | bytes 12582912 | tf_op jit(solution)/shard_map/pallas_call | solution.py:224
  24.2 0.0 copy-done
  24.3 0.0 copy-start.2
  24.3 0.0 copy-start.3
  24.3 0.2 shard_map.71
  24.5 0.0 collective-permute-done.5.before_ref
  24.5 0.2 shard_map.72
  24.7 0.1 collective-permute-start.8
  24.8 2.1 %collective-permute-start.7 = (f32[32,256]{1,0:T(8,128)S(1)}, f32[32,256]{1,0:T(8,128)S(1)}, u32[]{:S(2)}, u32[]{:S(2)}) collective-permute-start(f32[32,256]{1,0:T(8,128)S(1)} %get-tuple-element.23), channel_id=1, source_target_pairs={{0,2},{1,3},{2,0},{3,1},{4,6},{5,7},{6,4},{7,5},{8,10},{9,11},{10,... | collective-permute-start | bytes 98312 | tf_op jit(solution)/shard_map/ppermute | solution.py:237
  27.0 0.5 collective-permute-start.6
  27.5 0.1 collective-permute-done.8
  27.6 1.2 %collective-permute-done.7 = f32[32,256]{1,0:T(8,128)S(1)} collective-permute-done((f32[32,256]{1,0:T(8,128)S(1)}, f32[32,256]{1,0:T(8,128)S(1)}, u32[]{:S(2)}, u32[]{:S(2)}) %collective-permute-start.7) | collective-permute-done | bytes 32800 | tf_op jit(solution)/shard_map/ppermute | solution.py:237
  28.8 1.3 %collective-permute-done.6 = f32[32,256]{1,0:T(8,128)S(1)} collective-permute-done((f32[32,256]{1,0:T(8,128)S(1)}, f32[32,256]{1,0:T(8,128)S(1)}, u32[]{:S(2)}, u32[]{:S(2)}) %collective-permute-start.6) | collective-permute-done | bytes 32800 | tf_op jit(solution)/shard_map/ppermute | solution.py:237
  30.1 2.8 %collective-permute-start.11 = (f32[32,256]{1,0:T(8,128)S(1)}, f32[32,256]{1,0:T(8,128)S(1)}, u32[]{:S(2)}, u32[]{:S(2)}) collective-permute-start(f32[32,256]{1,0:T(8,128)S(1)} %add_add_fusion.refs_0_), channel_id=1, source_target_pairs={{0,12},{4,8},{8,4},{12,0},{1,13},{5,9},{9,5},{13,1},{2,14},{6,10},... | collective-permute-start | bytes 98312 | tf_op jit(solution)/shard_map/ppermute | solution.py:238
  32.9 0.3 collective-permute-start.10
  33.3 0.3 collective-permute-start.9
  33.6 0.6 collective-permute-done.11.refs_3_
  34.2 3.0 %collective-permute-done.10.refs_2_ = f32[32,256]{1,0:T(8,128)S(1)} collective-permute-done((f32[32,256]{1,0:T(8,128)S(1)}, f32[32,256]{1,0:T(8,128)S(1)}, u32[]{:S(2)}, u32[]{:S(2)}) %collective-permute-start.10) | collective-permute-done | bytes 32800 | tf_op jit(solution)/shard_map/ppermute | solution.py:238
  37.2 0.0 collective-permute-done.9.refs_1_
  37.2 0.0 copy-done.2
  37.2 0.0 copy-done.3
  37.2 0.9 %shard_map.73 = (f32[32,256]{1,0:T(8,128)S(1)}, f32[32,256]{1,0:T(8,128)S(1)}, f32[64,256]{1,0:T(8,128)S(1)}) custom-call(f32[32,256]{1,0:T(8,128)S(1)} %add_add_fusion.refs_0_, f32[32,256]{1,0:T(8,128)S(1)} %collective-permute-done.9.refs_1_, f32[32,256]{1,0:T(8,128)S(1)} %collective-permute-done.10.refs_2_, f32[32,256]{1,0:T(8,128)S(1)} %collective-permute-done.11.refs_3_, ...), custom_call_target="tpu_custom_call" | custom-call | flops 1048576 | bytes 2097152 | tf_op jit(solution)/shard_map/pallas_call | solution.py:243
  38.1 3.1 %collective-permute-start.12 = (f32[64,256]{1,0:T(8,128)S(1)}, f32[64,256]{1,0:T(8,128)S(1)}, u32[]{:S(2)}, u32[]{:S(2)}) collective-permute-start(f32[64,256]{1,0:T(8,128)S(1)} %get-tuple-element.27), channel_id=1, source_target_pairs={{0,16},{16,0},{1,17},{17,1},{2,18},{18,2},{3,19},{19,3},{4,20},{20... | collective-permute-start | bytes 196616 | tf_op jit(solution)/shard_map/ppermute | solution.py:246
  41.2 0.2 shard_map.74
  41.4 0.7 %collective-permute-done.12 = f32[64,256]{1,0:T(8,128)S(1)} collective-permute-done((f32[64,256]{1,0:T(8,128)S(1)}, f32[64,256]{1,0:T(8,128)S(1)}, u32[]{:S(2)}, u32[]{:S(2)}) %collective-permute-start.12) | collective-permute-done | bytes 65568 | tf_op jit(solution)/shard_map/ppermute | solution.py:246
  42.1 4.6 %collective-permute-start.13 = (f32[64,256]{1,0:T(8,128)S(1)}, f32[64,256]{1,0:T(8,128)S(1)}, u32[]{:S(2)}, u32[]{:S(2)}) collective-permute-start(f32[64,256]{1,0:T(8,128)S(1)} %add.61), channel_id=1, source_target_pairs={{0,32},{32,0},{1,33},{33,1},{2,34},{34,2},{3,35},{35,3},{4,36},{36... | collective-permute-start | bytes 196616 | tf_op jit(solution)/shard_map/ppermute | solution.py:192
  46.7 4.3 %collective-permute-done.13 = f32[64,256]{1,0:T(8,128)S(1)} collective-permute-done((f32[64,256]{1,0:T(8,128)S(1)}, f32[64,256]{1,0:T(8,128)S(1)}, u32[]{:S(2)}, u32[]{:S(2)}) %collective-permute-start.13) | collective-permute-done | bytes 65568 | tf_op jit(solution)/shard_map/ppermute | solution.py:192
  51.0 1.2 %collective-permute-start.16 = (f32[64,256]{1,0:T(8,128)S(1)}, f32[64,256]{1,0:T(8,128)S(1)}, u32[]{:S(2)}, u32[]{:S(2)}) collective-permute-start(f32[64,256]{1,0:T(8,128)S(1)} %add.62), channel_id=1, source_target_pairs={{0,192},{64,128},{128,64},{192,0},{1,193},{65,129},{129,65},{193,1... | collective-permute-start | bytes 196616 | tf_op jit(solution)/shard_map/ppermute | solution.py:194
  52.2 0.7 %collective-permute-start.15 = (f32[64,256]{1,0:T(8,128)S(1)}, f32[64,256]{1,0:T(8,128)S(1)}, u32[]{:S(2)}, u32[]{:S(2)}) collective-permute-start(f32[64,256]{1,0:T(8,128)S(1)} %add.62), channel_id=1, source_target_pairs={{0,128},{64,192},{128,0},{192,64},{1,129},{65,193},{129,1},{193,65... | collective-permute-start | bytes 196616 | tf_op jit(solution)/shard_map/ppermute | solution.py:194
  52.9 1.4 %collective-permute-start.14 = (f32[64,256]{1,0:T(8,128)S(1)}, f32[64,256]{1,0:T(8,128)S(1)}, u32[]{:S(2)}, u32[]{:S(2)}) collective-permute-start(f32[64,256]{1,0:T(8,128)S(1)} %add.62), channel_id=1, source_target_pairs={{0,64},{64,0},{128,192},{192,128},{1,65},{65,1},{129,193},{193,129... | collective-permute-start | bytes 196616 | tf_op jit(solution)/shard_map/ppermute | solution.py:194
  54.4 1.1 %collective-permute-done.16 = f32[64,256]{1,0:T(8,128)S(1)} collective-permute-done((f32[64,256]{1,0:T(8,128)S(1)}, f32[64,256]{1,0:T(8,128)S(1)}, u32[]{:S(2)}, u32[]{:S(2)}) %collective-permute-start.16) | collective-permute-done | bytes 65568 | tf_op jit(solution)/shard_map/ppermute | solution.py:194
  55.4 1.5 %collective-permute-done.15 = f32[64,256]{1,0:T(8,128)S(1)} collective-permute-done((f32[64,256]{1,0:T(8,128)S(1)}, f32[64,256]{1,0:T(8,128)S(1)}, u32[]{:S(2)}, u32[]{:S(2)}) %collective-permute-start.15) | collective-permute-done | bytes 65568 | tf_op jit(solution)/shard_map/ppermute | solution.py:194
  56.9 0.1 collective-permute-done.14
  57.1 2.5 %collective-permute-start.17 = (f32[64,256]{1,0:T(8,128)S(1)}, f32[64,256]{1,0:T(8,128)S(1)}, u32[]{:S(2)}, u32[]{:S(2)}) collective-permute-start(f32[64,256]{1,0:T(8,128)S(1)} %multiply_add_fusion.1), channel_id=1, source_target_pairs={{0,16},{16,0},{1,17},{17,1},{2,18},{18,2},{3,19},{19,3},{4,20},{20... | collective-permute-start | bytes 196616 | tf_op jit(solution)/shard_map/ppermute | solution.py:198
  59.5 0.7 %shard_map.78 = f32[16,32]{1,0:T(8,128)} custom-call(f32[32,256]{1,0:T(8,128)S(1)} %get-tuple-element.29.residual_ref), custom_call_target="tpu_custom_call" | custom-call | flops 32768 | bytes 65536 | tf_op jit(solution)/shard_map/pallas_call | solution.py:251
  60.2 1.0 %shard_map.75.known_ref = f32[2,32,64,256]{3,2,1,0:T(8,128)S(1)} custom-call(f32[1,256]{1,0:T(1,128)S(1)} %bitcast.17, f32[32,256]{1,0:T(8,128)S(1)} %get-tuple-element.25.back_ref, f32[64,256]{1,0:T(8,128)S(1)} %get-tuple-element.26.entered_ref.own_entered_ref, f32[64,256]{1,0:T(8,128)S(1)} %get-tuple-element.24.refs_7_.other_entered_ref, ...), custom_call_target="tpu_custom_call" | custom-call | flops 6291456 | bytes 12582912 | tf_op jit(solution)/shard_map/pallas_call | solution.py:248
  61.2 1.4 %shard_map.76.begun_hbm = f32[32,128,256]{2,1,0:T(8,128)} custom-call(f32[64,256]{1,0:T(8,128)S(1)} %get-tuple-element.30.after_ref, f32[1,256]{1,0:T(1,128)S(1)} %bitcast.18, f32[2,32,64,256]{3,2,1,0:T(8,128)S(1)} %shard_map.75.known_ref), custom_call_target="tpu_custom_call" | custom-call | flops 524288 | bytes 6291456 | tf_op jit(solution)/shard_map/pallas_call | solution.py:258
  62.6 0.0 collective-permute-done.17.after_ref
  62.6 1.4 %shard_map.77 = f32[32,128,256]{2,1,0:T(8,128)} custom-call(f32[64,256]{1,0:T(8,128)S(1)} %collective-permute-done.17.after_ref, f32[1,256]{1,0:T(1,128)S(1)} %bitcast.19, f32[2,32,64,256]{3,2,1,0:T(8,128)S(1)} %shard_map.75.known_ref, f32[32,128,256]{2,1,0:T(8,128)} %shard_map.76.begun_hbm), custom_call_target="tpu_custom_call", output_to_operand_aliasing={{}: (3, {})} | custom-call | flops 524288 | bytes 6291456 | tf_op jit(solution)/shard_map/pallas_call | solution.py:261
  (12 shorter events, 0.2 us)
Async XLA Ops:
  0.6 22.8 %copy-start.1 = (f32[256]{0:T(256)S(1)}, f32[256]{0:T(256)}, u32[]{:S(2)}) copy-start(f32[256]{0:T(256)} %param.7) | copy-start | bytes 3076
  2.2 22.0 %copy-start = (f32[128,256]{1,0:T(8,128)S(1)}, f32[128,256]{1,0:T(8,128)}, u32[]{:S(2)}) copy-start(f32[128,256]{1,0:T(8,128)} %entry_ref.3) | copy-start | bytes 393220
  2.3 2.4 %collective-permute-start = (f32[64,256]{1,0:T(8,128)S(1)}, f32[64,256]{1,0:T(8,128)S(1)}, u32[]{:S(2)}, u32[]{:S(2)}) collective-permute-start(f32[64,256]{1,0:T(8,128)S(1)} %get-tuple-element.18), channel_id=1, source_target_pairs={{0,16},{16,0},{1,17},{17,1},{2,18},{18,2},{3,19},{19,3},{4,20},{20... | collective-permute-start | bytes 196616 | tf_op jit(solution)/shard_map/ppermute | solution.py:220
  4.6 9.0 %collective-permute-start.1 = (f32[64,256]{1,0:T(8,128)S(1)}, f32[64,256]{1,0:T(8,128)S(1)}, u32[]{:S(2)}, u32[]{:S(2)}) collective-permute-start(f32[64,256]{1,0:T(8,128)S(1)} %add.51), channel_id=1, source_target_pairs={{0,32},{32,0},{1,33},{33,1},{2,34},{34,2},{3,35},{35,3},{4,36},{36... | collective-permute-start | bytes 196616 | tf_op jit(solution)/shard_map/ppermute | solution.py:192
  13.7 4.4 %collective-permute-start.4 = (f32[64,256]{1,0:T(8,128)S(1)}, f32[64,256]{1,0:T(8,128)S(1)}, u32[]{:S(2)}, u32[]{:S(2)}) collective-permute-start(f32[64,256]{1,0:T(8,128)S(1)} %add.52), channel_id=1, source_target_pairs={{0,192},{64,128},{128,64},{192,0},{1,193},{65,129},{129,65},{193,1... | collective-permute-start | bytes 196616 | tf_op jit(solution)/shard_map/ppermute | solution.py:194
  16.2 4.6 %collective-permute-start.3 = (f32[64,256]{1,0:T(8,128)S(1)}, f32[64,256]{1,0:T(8,128)S(1)}, u32[]{:S(2)}, u32[]{:S(2)}) collective-permute-start(f32[64,256]{1,0:T(8,128)S(1)} %add.52), channel_id=1, source_target_pairs={{0,128},{64,192},{128,0},{192,64},{1,129},{65,193},{129,1},{193,65... | collective-permute-start | bytes 196616 | tf_op jit(solution)/shard_map/ppermute | solution.py:194
  16.8 4.1 %collective-permute-start.2 = (f32[64,256]{1,0:T(8,128)S(1)}, f32[64,256]{1,0:T(8,128)S(1)}, u32[]{:S(2)}, u32[]{:S(2)}) collective-permute-start(f32[64,256]{1,0:T(8,128)S(1)} %add.52), channel_id=1, source_target_pairs={{0,64},{64,0},{128,192},{192,128},{1,65},{65,1},{129,193},{193,129... | collective-permute-start | bytes 196616 | tf_op jit(solution)/shard_map/ppermute | solution.py:194
  20.9 3.6 %collective-permute-start.5 = (f32[64,256]{1,0:T(8,128)S(1)}, f32[64,256]{1,0:T(8,128)S(1)}, u32[]{:S(2)}, u32[]{:S(2)}) collective-permute-start(f32[64,256]{1,0:T(8,128)S(1)} %multiply_add_fusion.4), channel_id=1, source_target_pairs={{0,16},{16,0},{1,17},{17,1},{2,18},{18,2},{3,19},{19,3},{4,20},{20... | collective-permute-start | bytes 196616 | tf_op jit(solution)/shard_map/ppermute | solution.py:198
  24.3 12.9 %copy-start.2 = (f32[32,256]{1,0:T(8,128)S(1)}, f32[32,256]{1,0:T(8,128)}, u32[]{:S(2)}) copy-start(f32[32,256]{1,0:T(8,128)} %refs_5_.1) | copy-start | bytes 98308
  24.3 12.9 %copy-start.3 = (f32[5]{0:T(128)S(1)}, f32[5]{0:T(128)}, u32[]{:S(2)}) copy-start(f32[5]{0:T(128)} %refs_4_.1) | copy-start | bytes 64
  24.7 2.9 %collective-permute-start.8 = (f32[32,256]{1,0:T(8,128)S(1)}, f32[32,256]{1,0:T(8,128)S(1)}, u32[]{:S(2)}, u32[]{:S(2)}) collective-permute-start(f32[32,256]{1,0:T(8,128)S(1)} %get-tuple-element.23), channel_id=1, source_target_pairs={{0,3},{1,2},{2,1},{3,0},{4,7},{5,6},{6,5},{7,4},{8,11},{9,10},{10,... | collective-permute-start | bytes 98312 | tf_op jit(solution)/shard_map/ppermute | solution.py:237
  24.8 3.9 %collective-permute-start.7 = (f32[32,256]{1,0:T(8,128)S(1)}, f32[32,256]{1,0:T(8,128)S(1)}, u32[]{:S(2)}, u32[]{:S(2)}) collective-permute-start(f32[32,256]{1,0:T(8,128)S(1)} %get-tuple-element.23), channel_id=1, source_target_pairs={{0,2},{1,3},{2,0},{3,1},{4,6},{5,7},{6,4},{7,5},{8,10},{9,11},{10,... | collective-permute-start | bytes 98312 | tf_op jit(solution)/shard_map/ppermute | solution.py:237
  27.0 3.1 %collective-permute-start.6 = (f32[32,256]{1,0:T(8,128)S(1)}, f32[32,256]{1,0:T(8,128)S(1)}, u32[]{:S(2)}, u32[]{:S(2)}) collective-permute-start(f32[32,256]{1,0:T(8,128)S(1)} %get-tuple-element.23), channel_id=1, source_target_pairs={{0,1},{1,0},{2,3},{3,2},{4,5},{5,4},{6,7},{7,6},{8,9},{9,8},{10,11... | collective-permute-start | bytes 98312 | tf_op jit(solution)/shard_map/ppermute | solution.py:237
  30.1 4.1 %collective-permute-start.11 = (f32[32,256]{1,0:T(8,128)S(1)}, f32[32,256]{1,0:T(8,128)S(1)}, u32[]{:S(2)}, u32[]{:S(2)}) collective-permute-start(f32[32,256]{1,0:T(8,128)S(1)} %add_add_fusion.refs_0_), channel_id=1, source_target_pairs={{0,12},{4,8},{8,4},{12,0},{1,13},{5,9},{9,5},{13,1},{2,14},{6,10},... | collective-permute-start | bytes 98312 | tf_op jit(solution)/shard_map/ppermute | solution.py:238
  32.9 4.3 %collective-permute-start.10 = (f32[32,256]{1,0:T(8,128)S(1)}, f32[32,256]{1,0:T(8,128)S(1)}, u32[]{:S(2)}, u32[]{:S(2)}) collective-permute-start(f32[32,256]{1,0:T(8,128)S(1)} %add_add_fusion.refs_0_), channel_id=1, source_target_pairs={{0,8},{4,12},{8,0},{12,4},{1,9},{5,13},{9,1},{13,5},{2,10},{6,14},... | collective-permute-start | bytes 98312 | tf_op jit(solution)/shard_map/ppermute | solution.py:238
  33.3 3.9 %collective-permute-start.9 = (f32[32,256]{1,0:T(8,128)S(1)}, f32[32,256]{1,0:T(8,128)S(1)}, u32[]{:S(2)}, u32[]{:S(2)}) collective-permute-start(f32[32,256]{1,0:T(8,128)S(1)} %add_add_fusion.refs_0_), channel_id=1, source_target_pairs={{0,4},{4,0},{8,12},{12,8},{1,5},{5,1},{9,13},{13,9},{2,6},{6,2},{1... | collective-permute-start | bytes 98312 | tf_op jit(solution)/shard_map/ppermute | solution.py:238
  38.1 4.0 %collective-permute-start.12 = (f32[64,256]{1,0:T(8,128)S(1)}, f32[64,256]{1,0:T(8,128)S(1)}, u32[]{:S(2)}, u32[]{:S(2)}) collective-permute-start(f32[64,256]{1,0:T(8,128)S(1)} %get-tuple-element.27), channel_id=1, source_target_pairs={{0,16},{16,0},{1,17},{17,1},{2,18},{18,2},{3,19},{19,3},{4,20},{20... | collective-permute-start | bytes 196616 | tf_op jit(solution)/shard_map/ppermute | solution.py:246
  42.1 8.9 %collective-permute-start.13 = (f32[64,256]{1,0:T(8,128)S(1)}, f32[64,256]{1,0:T(8,128)S(1)}, u32[]{:S(2)}, u32[]{:S(2)}) collective-permute-start(f32[64,256]{1,0:T(8,128)S(1)} %add.61), channel_id=1, source_target_pairs={{0,32},{32,0},{1,33},{33,1},{2,34},{34,2},{3,35},{35,3},{4,36},{36... | collective-permute-start | bytes 196616 | tf_op jit(solution)/shard_map/ppermute | solution.py:192
  51.0 4.4 %collective-permute-start.16 = (f32[64,256]{1,0:T(8,128)S(1)}, f32[64,256]{1,0:T(8,128)S(1)}, u32[]{:S(2)}, u32[]{:S(2)}) collective-permute-start(f32[64,256]{1,0:T(8,128)S(1)} %add.62), channel_id=1, source_target_pairs={{0,192},{64,128},{128,64},{192,0},{1,193},{65,129},{129,65},{193,1... | collective-permute-start | bytes 196616 | tf_op jit(solution)/shard_map/ppermute | solution.py:194
  52.2 4.7 %collective-permute-start.15 = (f32[64,256]{1,0:T(8,128)S(1)}, f32[64,256]{1,0:T(8,128)S(1)}, u32[]{:S(2)}, u32[]{:S(2)}) collective-permute-start(f32[64,256]{1,0:T(8,128)S(1)} %add.62), channel_id=1, source_target_pairs={{0,128},{64,192},{128,0},{192,64},{1,129},{65,193},{129,1},{193,65... | collective-permute-start | bytes 196616 | tf_op jit(solution)/shard_map/ppermute | solution.py:194
  52.9 4.1 %collective-permute-start.14 = (f32[64,256]{1,0:T(8,128)S(1)}, f32[64,256]{1,0:T(8,128)S(1)}, u32[]{:S(2)}, u32[]{:S(2)}) collective-permute-start(f32[64,256]{1,0:T(8,128)S(1)} %add.62), channel_id=1, source_target_pairs={{0,64},{64,0},{128,192},{192,128},{1,65},{65,1},{129,193},{193,129... | collective-permute-start | bytes 196616 | tf_op jit(solution)/shard_map/ppermute | solution.py:194
  57.1 5.5 %collective-permute-start.17 = (f32[64,256]{1,0:T(8,128)S(1)}, f32[64,256]{1,0:T(8,128)S(1)}, u32[]{:S(2)}, u32[]{:S(2)}) collective-permute-start(f32[64,256]{1,0:T(8,128)S(1)} %multiply_add_fusion.1), channel_id=1, source_target_pairs={{0,16},{16,0},{1,17},{17,1},{2,18},{18,2},{3,19},{19,3},{4,20},{20... | collective-permute-start | bytes 196616 | tf_op jit(solution)/shard_map/ppermute | solution.py:198

commit v3 on v2

--- a/solution.py
+++ b/solution.py
@@ -103,16 +103,20 @@
     imaged(1, before_ref, absorb_ref, entry_ref, emit_ref, entered_ref, part_ref, earlier_ref)
 
 
-def shifted(value, by):
-    width = value.shape[1]
-    source = lax.broadcasted_iota(jnp.int32, value.shape, 1) + by
-    moved = pltpu.roll(value, (-by) % width, 1)
-    return jnp.where((source >= 0) & (source < width), moved, 0.0)
-
-
-def blurred(value, taps_ref, sign):
-    terms = [taps_ref[k] * shifted(value, sign * (k - 2)) for k in (0, 1, 3, 4)]
-    return (taps_ref[2] * value + (terms[0] + terms[1])) + (terms[2] + terms[3])
+def product(left, right, contracted=0):
+    dims = (((1,), (contracted,)), ((), ()))
+    return lax.dot_general(left, right, dims, precision=lax.Precision.HIGHEST, preferred_element_type=F32)
+
+
+def band_body(scale, taps_ref, measured_ref, band_ref, both_ref, target_ref):
+    size = band_ref.shape
+    offset = lax.broadcasted_iota(jnp.int32, size, 0) - lax.broadcasted_iota(jnp.int32, size, 1)
+    band = jnp.zeros(size, F32)
+    for k in range(5):
+        band = jnp.where(offset == k - 2, taps_ref[k], band)
+    band_ref[...] = band * scale
+    both_ref[...] = product(band, band, 1) * scale
+    target_ref[...] = product(measured_ref[...], band, 1)
 
 
 def weighed(half, back_ref, emit_ref, entered_ref):
@@ -123,12 +127,10 @@
     return total * entered_ref[...]
 
 
-def adjoint_other_body(scale, s0, s1, s2, s3, taps_ref, measured_ref, emit_ref, entered_ref,
-                       residual_ref, back_ref, total_ref):
-    image = ((s0[...] + s1[...]) + (s2[...] + s3[...])) * scale
-    residual = blurred(image, taps_ref, 1) - measured_ref[...]
-    residual_ref[...] = residual
-    back_ref[...] = blurred(residual, taps_ref, -1)
+def adjoint_other_body(s0, s1, s2, s3, both_ref, target_ref, emit_ref, entered_ref, image_ref, back_ref, total_ref):
+    image = (s0[...] + s1[...]) + (s2[...] + s3[...])
+    image_ref[...] = image
+    back_ref[...] = product(image, both_ref[...]) - target_ref[...]
     total_ref[...] = weighed(1, back_ref, emit_ref, entered_ref)
 
 
@@ -136,10 +138,11 @@
     total_ref[...] = weighed(0, back_ref, emit_ref, entered_ref)
 
 
-def turn_body(residual_ref, columns_ref, turned_ref):
+def turn_body(image_ref, band_ref, measured_ref, columns_ref, turned_ref):
     width = columns_ref.shape[0]
     section = (lax.axis_index("y") * lax.axis_size("zl") + lax.axis_index("zl")) * width
-    turned_ref[...] = residual_ref[...].T
+    residual = product(image_ref[...], band_ref[...]) - measured_ref[...]
+    turned_ref[...] = residual.T
     columns_ref[...] = turned_ref[pl.ds(pl.multiple_of(section, 8), width), :]
 
 
@@ -184,6 +187,13 @@
     written(1, after_ref, absorb_ref, known_ref, out_hbm, out_ref, sems)
 
 
+def exchanged(value, axis):
+    rows = []
+    for k in (1, 2, 3):
+        rows.append(lax.ppermute(value, axis, xor(4, k)))
+    return rows
+
+
 def scanned(own, partner, flags, reverse):
     if reverse:
         flags = 1.0 - flags
@@ -191,7 +201,7 @@
     pair = own + partner
     crossed = lax.ppermute(pair, "zh", xor(2, 1))
     both = pair + crossed
-    rows = [lax.ppermute(both, "x", xor(4, k)) for k in (1, 2, 3)]
+    rows = exchanged(both, "x")
     base = flags[2:3] * rows[0] + flags[3:4] * rows[1] + flags[4:5] * rows[2] + late_z * crossed
     for_me = base + late_core * partner
     for_other = base + (1.0 - late_core) * own
@@ -224,6 +234,12 @@
     light, emit = call(
         local_body, (blocks, blocks), [VM] * 3, (VM, VM), 4 * size, 12 * size, size
     )(own_cells, other_cells, rate)
+    square = jax.ShapeDtypeStruct((height, height), F32)
+
+    def bands(*refs):
+        band_body(scale, *refs)
+
+    band, both, target = call(bands, (square, square, camera), [SM, VM], (VM,) * 3, 2**24, 2**20)(blur_taps, measured)
     before_own, before_other = scanned(own, partner, flags, False)
     own_entered, part = call(
         image_own_body, (half, camera), [VM] * 4, (VM, VM), size, 2 * size, count * height
@@ -232,26 +248,22 @@
         image_other_body, (half, camera), [VM] * 5, (VM, VM), size, 2 * size, count * height
     )(before_other, rate, entry_intensity, emit, part)
 
-    over_z = part
-    for k in (1, 2, 3):
-        over_z = over_z + lax.ppermute(part, "zl", xor(4, k))
-    sums = [over_z] + [lax.ppermute(over_z, "y", xor(4, k)) for k in (1, 2, 3)]
-
-    def adjoint_other(*refs):
-        adjoint_other_body(scale, *refs)
-
-    full_residual, back, other = call(
-        adjoint_other, (camera, camera, half), [VM] * 4 + [SM] + [VM] * 3, (VM,) * 3, size, 2 * size
-    )(*sums, blur_taps, measured, emit, other_entered)
+    rows = exchanged(part, "zl")
+    over_z = (part + rows[0]) + (rows[1] + rows[2])
+    sums = [over_z] + exchanged(over_z, "y")
+
+    image, back, other = call(
+        adjoint_other_body, (camera, camera, half), [VM] * 8, (VM,) * 3, size, 2 * size
+    )(*sums, both, target, emit, other_entered)
     partner = lax.ppermute(other, "core", xor(2, 1))
     own = call(adjoint_own_body, half, [VM] * 3, VM, size, 2 * size)(back, emit, own_entered)
     known = call(partial_body, blocks, [VM] * 6, VM, 6 * size, 12 * size)(
         rate, back, own_entered, other_entered, light, emit
     )
     columns = call(
-        turn_body, jax.ShapeDtypeStruct((width, beam), F32), [VM], VM, 32768, 65536,
+        turn_body, jax.ShapeDtypeStruct((width, beam), F32), [VM] * 3, VM, 32768, 65536,
         scratch=(pltpu.VMEM((height, beam), F32),),
-    )(full_residual)
+    )(image, band, measured)
     after_own, after_other = scanned(own, partner, flags, True)
     written_scratch = (pltpu.VMEM((beam, count, height), F32), copied)
     whole = jax.ShapeDtypeStruct((beam, depth, height), F32)

time: 65 us -> 67.4 us (1.037)
  the two profiles are of different devices: /device:TPU:65 before, /device:TPU:1 now
where the time goes in v3:
time: 67.4 us; the launch traced here: 67.2 us
  starting transfers between devices  38.1 us (57%)
  waiting for transfers between devices  17.2 us (26%)
  Pallas kernels  10.9 us (16%)
  between operations  0.83 us (1%)
    ppermute x12, starting transfers between devices, exchanged(): rows.append(lax.ppermute(value, axis, xor(4, k)))  15.8 us
    ppermute x12, waiting for transfers between devices, exchanged(): rows.append(lax.ppermute(value, axis, xor(4, k)))  11.9 us
    ppermute x2, starting transfers between devices, scanned(): crossed = lax.ppermute(pair, 'zh', xor(2, 1))  10.1 us
    ppermute x2, starting transfers between devices, local(): partner = lax.ppermute(other, 'core', xor(2, 1))  6.61 us
    ppermute x2, starting transfers between devices, scanned(): return (for_me, lax.ppermute(for_other, 'core', xor(2, 1)))  5.6 us
    ppermute x2, waiting for transfers between devices, scanned(): crossed = lax.ppermute(pair, 'zh', xor(2, 1))  4.63 us
    pallas_call x1, Pallas kernels, local(): call(load_other_body, (half_block, half, jax.ShapeDtypeStruct((8, height)...  1.6 us
    pallas_call x1, Pallas kernels, local(): call(load_own_body, (half_block, half), [HBM], (VM, VM), size // 2, 4 * s...  1.59 us
  transfers between devices with their start and end apart: 18, of which 10 were waited for; matrix products, arithmetic and copies ran while one was open for 0% of the time, Pallas kernels for 11%

profile of v3, /device:TPU:1, one launch (start us, length us, event | category | flops | bytes accessed | tf_op | source)
XLA Modules:
  0.0 67.2 jit_solution(15935673281067117924)
XLA Ops:
  0.6 0.0 copy-start.1
  0.6 1.6 %shard_map.68 = (f32[32,64,256]{2,1,0:T(8,128)S(1)}, f32[64,256]{1,0:T(8,128)S(1)}, f32[8,256]{1,0:T(8,128)S(1)}) custom-call(f32[32,128,256]{2,1,0:T(8,128)} %c_hbm.3), custom_call_target="tpu_custom_call" | custom-call | flops 524288 | bytes 4194304 | tf_op jit(solution)/shard_map/pallas_call | solution.py:226
  2.2 0.0 copy-start
  2.3 3.3 %collective-permute-start = (f32[64,256]{1,0:T(8,128)S(1)}, f32[64,256]{1,0:T(8,128)S(1)}, u32[]{:S(2)}, u32[]{:S(2)}) collective-permute-start(f32[64,256]{1,0:T(8,128)S(1)} %get-tuple-element.21), channel_id=1, source_target_pairs={{0,16},{16,0},{1,17},{17,1},{2,18},{18,2},{3,19},{19,3},{4,20},{20... | collective-permute-start | bytes 196616 | tf_op jit(solution)/shard_map/ppermute | solution.py:230
  5.5 1.6 %shard_map.69 = (f32[32,64,256]{2,1,0:T(8,128)S(1)}, f32[64,256]{1,0:T(8,128)S(1)}) custom-call(f32[32,128,256]{2,1,0:T(8,128)} %c_hbm.3), custom_call_target="tpu_custom_call" | custom-call | flops 524288 | bytes 4194304 | tf_op jit(solution)/shard_map/pallas_call | solution.py:231
  7.1 0.0 collective-permute-done
  7.2 5.3 %collective-permute-start.1 = (f32[64,256]{1,0:T(8,128)S(1)}, f32[64,256]{1,0:T(8,128)S(1)}, u32[]{:S(2)}, u32[]{:S(2)}) collective-permute-start(f32[64,256]{1,0:T(8,128)S(1)} %add.51), channel_id=1, source_target_pairs={{0,32},{32,0},{1,33},{33,1},{2,34},{34,2},{3,35},{35,3},{4,36},{36... | collective-permute-start | bytes 196616 | tf_op jit(solution)/shard_map/ppermute | solution.py:202
  12.5 2.3 %collective-permute-done.1 = f32[64,256]{1,0:T(8,128)S(1)} collective-permute-done((f32[64,256]{1,0:T(8,128)S(1)}, f32[64,256]{1,0:T(8,128)S(1)}, u32[]{:S(2)}, u32[]{:S(2)}) %collective-permute-start.1) | collective-permute-done | bytes 65568 | tf_op jit(solution)/shard_map/ppermute | solution.py:202
  14.8 1.4 %collective-permute-start.2 = (f32[64,256]{1,0:T(8,128)S(1)}, f32[64,256]{1,0:T(8,128)S(1)}, u32[]{:S(2)}, u32[]{:S(2)}) collective-permute-start(f32[64,256]{1,0:T(8,128)S(1)} %add.52), channel_id=1, source_target_pairs={{0,64},{64,0},{128,192},{192,128},{1,65},{65,1},{129,193},{193,129... | collective-permute-start | bytes 196616 | tf_op jit(solution)/shard_map/ppermute | solution.py:193
  16.2 2.5 %collective-permute-start.3 = (f32[64,256]{1,0:T(8,128)S(1)}, f32[64,256]{1,0:T(8,128)S(1)}, u32[]{:S(2)}, u32[]{:S(2)}) collective-permute-start(f32[64,256]{1,0:T(8,128)S(1)} %add.52), channel_id=1, source_target_pairs={{0,128},{64,192},{128,0},{192,64},{1,129},{65,193},{129,1},{193,65... | collective-permute-start | bytes 196616 | tf_op jit(solution)/shard_map/ppermute | solution.py:193
  18.7 0.1 collective-permute-start.4
  18.8 0.0 collective-permute-done.2
  18.8 2.5 %collective-permute-done.3 = f32[64,256]{1,0:T(8,128)S(1)} collective-permute-done((f32[64,256]{1,0:T(8,128)S(1)}, f32[64,256]{1,0:T(8,128)S(1)}, u32[]{:S(2)}, u32[]{:S(2)}) %collective-permute-start.3) | collective-permute-done | bytes 65568 | tf_op jit(solution)/shard_map/ppermute | solution.py:193
  21.3 1.9 %collective-permute-done.4 = f32[64,256]{1,0:T(8,128)S(1)} collective-permute-done((f32[64,256]{1,0:T(8,128)S(1)}, f32[64,256]{1,0:T(8,128)S(1)}, u32[]{:S(2)}, u32[]{:S(2)}) %collective-permute-start.4) | collective-permute-done | bytes 65568 | tf_op jit(solution)/shard_map/ppermute | solution.py:193
  23.2 2.4 %collective-permute-start.5 = (f32[64,256]{1,0:T(8,128)S(1)}, f32[64,256]{1,0:T(8,128)S(1)}, u32[]{:S(2)}, u32[]{:S(2)}) collective-permute-start(f32[64,256]{1,0:T(8,128)S(1)} %multiply_add_fusion.4), channel_id=1, source_target_pairs={{0,16},{16,0},{1,17},{17,1},{2,18},{18,2},{3,19},{19,3},{4,20},{20... | collective-permute-start | bytes 196616 | tf_op jit(solution)/shard_map/ppermute | solution.py:208
  25.5 0.0 copy-done.1
  25.6 0.8 %shard_map.70 = (f32[2,32,64,256]{3,2,1,0:T(8,128)S(1)}, f32[2,32,64,256]{3,2,1,0:T(8,128)S(1)}) custom-call(f32[32,64,256]{2,1,0:T(8,128)S(1)} %get-tuple-element.22.own_ref, f32[32,64,256]{2,1,0:T(8,128)S(1)} %get-tuple-element.23.other_ref, f32[1,256]{1,0:T(1,128)S(1)} %bitcast.14), custom_call_target="tpu_custom_call" | custom-call | flops 4194304 | bytes 12582912 | tf_op jit(solution)/shard_map/pallas_call | solution.py:234
  26.3 0.0 copy-done
  26.3 0.0 copy-start.2
  26.3 0.0 copy-start.3
  26.4 0.2 shard_map.71
  26.6 0.0 collective-permute-done.5.before_ref
  26.6 0.2 shard_map.72
  26.8 0.7 %collective-permute-start.6 = (f32[32,256]{1,0:T(8,128)S(1)}, f32[32,256]{1,0:T(8,128)S(1)}, u32[]{:S(2)}, u32[]{:S(2)}) collective-permute-start(f32[32,256]{1,0:T(8,128)S(1)} %get-tuple-element.26), channel_id=1, source_target_pairs={{0,1},{1,0},{2,3},{3,2},{4,5},{5,4},{6,7},{7,6},{8,9},{9,8},{10,11... | collective-permute-start | bytes 98312 | tf_op jit(solution)/shard_map/ppermute | solution.py:193
  27.6 2.3 %collective-permute-start.7 = (f32[32,256]{1,0:T(8,128)S(1)}, f32[32,256]{1,0:T(8,128)S(1)}, u32[]{:S(2)}, u32[]{:S(2)}) collective-permute-start(f32[32,256]{1,0:T(8,128)S(1)} %get-tuple-element.26), channel_id=1, source_target_pairs={{0,2},{1,3},{2,0},{3,1},{4,6},{5,7},{6,4},{7,5},{8,10},{9,11},{10,... | collective-permute-start | bytes 98312 | tf_op jit(solution)/shard_map/ppermute | solution.py:193
  29.9 1.1 %collective-permute-start.8 = (f32[32,256]{1,0:T(8,128)S(1)}, f32[32,256]{1,0:T(8,128)S(1)}, u32[]{:S(2)}, u32[]{:S(2)}) collective-permute-start(f32[32,256]{1,0:T(8,128)S(1)} %get-tuple-element.26), channel_id=1, source_target_pairs={{0,3},{1,2},{2,1},{3,0},{4,7},{5,6},{6,5},{7,4},{8,11},{9,10},{10,... | collective-permute-start | bytes 98312 | tf_op jit(solution)/shard_map/ppermute | solution.py:193
  31.0 0.0 collective-permute-done.6
  31.0 0.2 collective-permute-done.7
  31.2 3.2 %collective-permute-done.8 = f32[32,256]{1,0:T(8,128)S(1)} collective-permute-done((f32[32,256]{1,0:T(8,128)S(1)}, f32[32,256]{1,0:T(8,128)S(1)}, u32[]{:S(2)}, u32[]{:S(2)}) %collective-permute-start.8) | collective-permute-done | bytes 32800 | tf_op jit(solution)/shard_map/ppermute | solution.py:193
  34.5 3.0 %collective-permute-start.10 = (f32[32,256]{1,0:T(8,128)S(1)}, f32[32,256]{1,0:T(8,128)S(1)}, u32[]{:S(2)}, u32[]{:S(2)}) collective-permute-start(f32[32,256]{1,0:T(8,128)S(1)} %add_add_fusion.s0), channel_id=1, source_target_pairs={{0,8},{4,12},{8,0},{12,4},{1,9},{5,13},{9,1},{13,5},{2,10},{6,14},... | collective-permute-start | bytes 98312 | tf_op jit(solution)/shard_map/ppermute | solution.py:193
  37.5 0.8 %collective-permute-start.11 = (f32[32,256]{1,0:T(8,128)S(1)}, f32[32,256]{1,0:T(8,128)S(1)}, u32[]{:S(2)}, u32[]{:S(2)}) collective-permute-start(f32[32,256]{1,0:T(8,128)S(1)} %add_add_fusion.s0), channel_id=1, source_target_pairs={{0,12},{4,8},{8,4},{12,0},{1,13},{5,9},{9,5},{13,1},{2,14},{6,10},... | collective-permute-start | bytes 98312 | tf_op jit(solution)/shard_map/ppermute | solution.py:193
  38.3 0.0 collective-permute-start.9
  38.3 0.0 copy-done.2
  38.3 0.0 copy-done.3
  38.3 1.1 %shard_map.73 = (f32[256,256]{1,0:T(8,128)S(1)}, f32[256,256]{1,0:T(8,128)S(1)}, f32[32,256]{1,0:T(8,128)S(1)}) custom-call(f32[5]{0:T(128)S(1)} %copy-done.3, f32[32,256]{1,0:T(8,128)S(1)} %copy-done.2), custom_call_target="tpu_custom_call" | custom-call | flops 16777216 | bytes 1048576 | tf_op jit(solution)/shard_map/pallas_call | solution.py:242
  39.4 0.0 collective-permute-done.10.s2
  39.4 2.1 %collective-permute-done.11.s3 = f32[32,256]{1,0:T(8,128)S(1)} collective-permute-done((f32[32,256]{1,0:T(8,128)S(1)}, f32[32,256]{1,0:T(8,128)S(1)}, u32[]{:S(2)}, u32[]{:S(2)}) %collective-permute-start.11) | collective-permute-done | bytes 32800 | tf_op jit(solution)/shard_map/ppermute | solution.py:193
  41.6 0.0 collective-permute-done.9.s1
  41.6 0.4 shard_map.74
  42.0 3.3 %collective-permute-start.12 = (f32[64,256]{1,0:T(8,128)S(1)}, f32[64,256]{1,0:T(8,128)S(1)}, u32[]{:S(2)}, u32[]{:S(2)}) collective-permute-start(f32[64,256]{1,0:T(8,128)S(1)} %get-tuple-element.32), channel_id=1, source_target_pairs={{0,16},{16,0},{1,17},{17,1},{2,18},{18,2},{3,19},{19,3},{4,20},{20... | collective-permute-start | bytes 196616 | tf_op jit(solution)/shard_map/ppermute | solution.py:258
  45.3 0.2 shard_map.75
  45.5 0.7 collective-permute-done.12
  46.2 4.8 %collective-permute-start.13 = (f32[64,256]{1,0:T(8,128)S(1)}, f32[64,256]{1,0:T(8,128)S(1)}, u32[]{:S(2)}, u32[]{:S(2)}) collective-permute-start(f32[64,256]{1,0:T(8,128)S(1)} %add.61), channel_id=1, source_target_pairs={{0,32},{32,0},{1,33},{33,1},{2,34},{34,2},{3,35},{35,3},{4,36},{36... | collective-permute-start | bytes 196616 | tf_op jit(solution)/shard_map/ppermute | solution.py:202
  51.0 2.3 %collective-permute-done.13 = f32[64,256]{1,0:T(8,128)S(1)} collective-permute-done((f32[64,256]{1,0:T(8,128)S(1)}, f32[64,256]{1,0:T(8,128)S(1)}, u32[]{:S(2)}, u32[]{:S(2)}) %collective-permute-start.13) | collective-permute-done | bytes 65568 | tf_op jit(solution)/shard_map/ppermute | solution.py:202
  53.3 0.1 collective-permute-start.14
  53.4 1.4 %collective-permute-start.15 = (f32[64,256]{1,0:T(8,128)S(1)}, f32[64,256]{1,0:T(8,128)S(1)}, u32[]{:S(2)}, u32[]{:S(2)}) collective-permute-start(f32[64,256]{1,0:T(8,128)S(1)} %add.62), channel_id=1, source_target_pairs={{0,128},{64,192},{128,0},{192,64},{1,129},{65,193},{129,1},{193,65... | collective-permute-start | bytes 196616 | tf_op jit(solution)/shard_map/ppermute | solution.py:193
  54.8 2.5 %collective-permute-start.16 = (f32[64,256]{1,0:T(8,128)S(1)}, f32[64,256]{1,0:T(8,128)S(1)}, u32[]{:S(2)}, u32[]{:S(2)}) collective-permute-start(f32[64,256]{1,0:T(8,128)S(1)} %add.62), channel_id=1, source_target_pairs={{0,192},{64,128},{128,64},{192,0},{1,193},{65,129},{129,65},{193,1... | collective-permute-start | bytes 196616 | tf_op jit(solution)/shard_map/ppermute | solution.py:193
  57.3 0.0 collective-permute-done.14
  57.3 1.3 %collective-permute-done.15 = f32[64,256]{1,0:T(8,128)S(1)} collective-permute-done((f32[64,256]{1,0:T(8,128)S(1)}, f32[64,256]{1,0:T(8,128)S(1)}, u32[]{:S(2)}, u32[]{:S(2)}) %collective-permute-start.15) | collective-permute-done | bytes 65568 | tf_op jit(solution)/shard_map/ppermute | solution.py:193
  58.6 0.6 collective-permute-done.16
  59.2 3.2 %collective-permute-start.17 = (f32[64,256]{1,0:T(8,128)S(1)}, f32[64,256]{1,0:T(8,128)S(1)}, u32[]{:S(2)}, u32[]{:S(2)}) collective-permute-start(f32[64,256]{1,0:T(8,128)S(1)} %multiply_add_fusion.1), channel_id=1, source_target_pairs={{0,16},{16,0},{1,17},{17,1},{2,18},{18,2},{3,19},{19,3},{4,20},{20... | collective-permute-start | bytes 196616 | tf_op jit(solution)/shard_map/ppermute | solution.py:208
  62.5 0.9 %shard_map.79 = f32[16,32]{1,0:T(8,128)} custom-call(f32[32,256]{1,0:T(8,128)S(1)} %get-tuple-element.34.image_ref, f32[256,256]{1,0:T(8,128)S(1)} %get-tuple-element.35.band_ref, f32[32,256]{1,0:T(8,128)S(1)} %copy-done.2), custom_call_target="tpu_custom_call" | custom-call | flops 32768 | bytes 65536 | tf_op jit(solution)/shard_map/pallas_call | solution.py:263
  63.4 1.0 %shard_map.76.known_ref = f32[2,32,64,256]{3,2,1,0:T(8,128)S(1)} custom-call(f32[1,256]{1,0:T(1,128)S(1)} %bitcast.17, f32[32,256]{1,0:T(8,128)S(1)} %get-tuple-element.30.back_ref, f32[64,256]{1,0:T(8,128)S(1)} %get-tuple-element.31.entered_ref.own_entered_ref, f32[64,256]{1,0:T(8,128)S(1)} %get-tuple-element.29.entered_ref.other_entered_ref, ...), custom_call_target="tpu_custom_call" | custom-call | flops 6291456 | bytes 12582912 | tf_op jit(solution)/shard_map/pallas_call | solution.py:260
  64.4 1.4 %shard_map.77.begun_hbm = f32[32,128,256]{2,1,0:T(8,128)} custom-call(f32[64,256]{1,0:T(8,128)S(1)} %get-tuple-element.36.after_ref, f32[1,256]{1,0:T(1,128)S(1)} %bitcast.18, f32[2,32,64,256]{3,2,1,0:T(8,128)S(1)} %shard_map.76.known_ref), custom_call_target="tpu_custom_call" | custom-call | flops 524288 | bytes 6291456 | tf_op jit(solution)/shard_map/pallas_call | solution.py:270
  65.8 0.0 collective-permute-done.17.after_ref
  65.8 1.4 %shard_map.78 = f32[32,128,256]{2,1,0:T(8,128)} custom-call(f32[64,256]{1,0:T(8,128)S(1)} %collective-permute-done.17.after_ref, f32[1,256]{1,0:T(1,128)S(1)} %bitcast.19, f32[2,32,64,256]{3,2,1,0:T(8,128)S(1)} %shard_map.76.known_ref, f32[32,128,256]{2,1,0:T(8,128)} %shard_map.77.begun_hbm), custom_call_target="tpu_custom_call", output_to_operand_aliasing={{}: (3, {})} | custom-call | flops 524288 | bytes 6291456 | tf_op jit(solution)/shard_map/pallas_call | solution.py:273
  (12 shorter events, 0.2 us)
Async XLA Ops:
  0.6 24.9 %copy-start.1 = (f32[256]{0:T(256)S(1)}, f32[256]{0:T(256)}, u32[]{:S(2)}) copy-start(f32[256]{0:T(256)} %param.7) | copy-start | bytes 3076
  2.2 24.1 %copy-start = (f32[128,256]{1,0:T(8,128)S(1)}, f32[128,256]{1,0:T(8,128)}, u32[]{:S(2)}) copy-start(f32[128,256]{1,0:T(8,128)} %entry_ref.3) | copy-start | bytes 393220
  2.3 4.9 %collective-permute-start = (f32[64,256]{1,0:T(8,128)S(1)}, f32[64,256]{1,0:T(8,128)S(1)}, u32[]{:S(2)}, u32[]{:S(2)}) collective-permute-start(f32[64,256]{1,0:T(8,128)S(1)} %get-tuple-element.21), channel_id=1, source_target_pairs={{0,16},{16,0},{1,17},{17,1},{2,18},{18,2},{3,19},{19,3},{4,20},{20... | collective-permute-start | bytes 196616 | tf_op jit(solution)/shard_map/ppermute | solution.py:230
  7.2 7.6 %collective-permute-start.1 = (f32[64,256]{1,0:T(8,128)S(1)}, f32[64,256]{1,0:T(8,128)S(1)}, u32[]{:S(2)}, u32[]{:S(2)}) collective-permute-start(f32[64,256]{1,0:T(8,128)S(1)} %add.51), channel_id=1, source_target_pairs={{0,32},{32,0},{1,33},{33,1},{2,34},{34,2},{3,35},{35,3},{4,36},{36... | collective-permute-start | bytes 196616 | tf_op jit(solution)/shard_map/ppermute | solution.py:202
  14.8 4.0 %collective-permute-start.2 = (f32[64,256]{1,0:T(8,128)S(1)}, f32[64,256]{1,0:T(8,128)S(1)}, u32[]{:S(2)}, u32[]{:S(2)}) collective-permute-start(f32[64,256]{1,0:T(8,128)S(1)} %add.52), channel_id=1, source_target_pairs={{0,64},{64,0},{128,192},{192,128},{1,65},{65,1},{129,193},{193,129... | collective-permute-start | bytes 196616 | tf_op jit(solution)/shard_map/ppermute | solution.py:193
  16.2 5.0 %collective-permute-start.3 = (f32[64,256]{1,0:T(8,128)S(1)}, f32[64,256]{1,0:T(8,128)S(1)}, u32[]{:S(2)}, u32[]{:S(2)}) collective-permute-start(f32[64,256]{1,0:T(8,128)S(1)} %add.52), channel_id=1, source_target_pairs={{0,128},{64,192},{128,0},{192,64},{1,129},{65,193},{129,1},{193,65... | collective-permute-start | bytes 196616 | tf_op jit(solution)/shard_map/ppermute | solution.py:193
  18.7 4.5 %collective-permute-start.4 = (f32[64,256]{1,0:T(8,128)S(1)}, f32[64,256]{1,0:T(8,128)S(1)}, u32[]{:S(2)}, u32[]{:S(2)}) collective-permute-start(f32[64,256]{1,0:T(8,128)S(1)} %add.52), channel_id=1, source_target_pairs={{0,192},{64,128},{128,64},{192,0},{1,193},{65,129},{129,65},{193,1... | collective-permute-start | bytes 196616 | tf_op jit(solution)/shard_map/ppermute | solution.py:193
  23.2 3.4 %collective-permute-start.5 = (f32[64,256]{1,0:T(8,128)S(1)}, f32[64,256]{1,0:T(8,128)S(1)}, u32[]{:S(2)}, u32[]{:S(2)}) collective-permute-start(f32[64,256]{1,0:T(8,128)S(1)} %multiply_add_fusion.4), channel_id=1, source_target_pairs={{0,16},{16,0},{1,17},{17,1},{2,18},{18,2},{3,19},{19,3},{4,20},{20... | collective-permute-start | bytes 196616 | tf_op jit(solution)/shard_map/ppermute | solution.py:208
  26.3 11.9 %copy-start.2 = (f32[32,256]{1,0:T(8,128)S(1)}, f32[32,256]{1,0:T(8,128)}, u32[]{:S(2)}) copy-start(f32[32,256]{1,0:T(8,128)} %measured_ref.1) | copy-start | bytes 98308
  26.3 11.9 %copy-start.3 = (f32[5]{0:T(128)S(1)}, f32[5]{0:T(128)}, u32[]{:S(2)}) copy-start(f32[5]{0:T(128)} %refs_0_.1) | copy-start | bytes 64
  26.8 4.2 %collective-permute-start.6 = (f32[32,256]{1,0:T(8,128)S(1)}, f32[32,256]{1,0:T(8,128)S(1)}, u32[]{:S(2)}, u32[]{:S(2)}) collective-permute-start(f32[32,256]{1,0:T(8,128)S(1)} %get-tuple-element.26), channel_id=1, source_target_pairs={{0,1},{1,0},{2,3},{3,2},{4,5},{5,4},{6,7},{7,6},{8,9},{9,8},{10,11... | collective-permute-start | bytes 98312 | tf_op jit(solution)/shard_map/ppermute | solution.py:193
  27.6 3.7 %collective-permute-start.7 = (f32[32,256]{1,0:T(8,128)S(1)}, f32[32,256]{1,0:T(8,128)S(1)}, u32[]{:S(2)}, u32[]{:S(2)}) collective-permute-start(f32[32,256]{1,0:T(8,128)S(1)} %get-tuple-element.26), channel_id=1, source_target_pairs={{0,2},{1,3},{2,0},{3,1},{4,6},{5,7},{6,4},{7,5},{8,10},{9,11},{10,... | collective-permute-start | bytes 98312 | tf_op jit(solution)/shard_map/ppermute | solution.py:193
  29.9 4.6 %collective-permute-start.8 = (f32[32,256]{1,0:T(8,128)S(1)}, f32[32,256]{1,0:T(8,128)S(1)}, u32[]{:S(2)}, u32[]{:S(2)}) collective-permute-start(f32[32,256]{1,0:T(8,128)S(1)} %get-tuple-element.26), channel_id=1, source_target_pairs={{0,3},{1,2},{2,1},{3,0},{4,7},{5,6},{6,5},{7,4},{8,11},{9,10},{10,... | collective-permute-start | bytes 98312 | tf_op jit(solution)/shard_map/ppermute | solution.py:193
  34.5 4.9 %collective-permute-start.10 = (f32[32,256]{1,0:T(8,128)S(1)}, f32[32,256]{1,0:T(8,128)S(1)}, u32[]{:S(2)}, u32[]{:S(2)}) collective-permute-start(f32[32,256]{1,0:T(8,128)S(1)} %add_add_fusion.s0), channel_id=1, source_target_pairs={{0,8},{4,12},{8,0},{12,4},{1,9},{5,13},{9,1},{13,5},{2,10},{6,14},... | collective-permute-start | bytes 98312 | tf_op jit(solution)/shard_map/ppermute | solution.py:193
  37.5 4.1 %collective-permute-start.11 = (f32[32,256]{1,0:T(8,128)S(1)}, f32[32,256]{1,0:T(8,128)S(1)}, u32[]{:S(2)}, u32[]{:S(2)}) collective-permute-start(f32[32,256]{1,0:T(8,128)S(1)} %add_add_fusion.s0), channel_id=1, source_target_pairs={{0,12},{4,8},{8,4},{12,0},{1,13},{5,9},{9,5},{13,1},{2,14},{6,10},... | collective-permute-start | bytes 98312 | tf_op jit(solution)/shard_map/ppermute | solution.py:193
  38.3 3.3 %collective-permute-start.9 = (f32[32,256]{1,0:T(8,128)S(1)}, f32[32,256]{1,0:T(8,128)S(1)}, u32[]{:S(2)}, u32[]{:S(2)}) collective-permute-start(f32[32,256]{1,0:T(8,128)S(1)} %add_add_fusion.s0), channel_id=1, source_target_pairs={{0,4},{4,0},{8,12},{12,8},{1,5},{5,1},{9,13},{13,9},{2,6},{6,2},{1... | collective-permute-start | bytes 98312 | tf_op jit(solution)/shard_map/ppermute | solution.py:193
  42.0 4.2 %collective-permute-start.12 = (f32[64,256]{1,0:T(8,128)S(1)}, f32[64,256]{1,0:T(8,128)S(1)}, u32[]{:S(2)}, u32[]{:S(2)}) collective-permute-start(f32[64,256]{1,0:T(8,128)S(1)} %get-tuple-element.32), channel_id=1, source_target_pairs={{0,16},{16,0},{1,17},{17,1},{2,18},{18,2},{3,19},{19,3},{4,20},{20... | collective-permute-start | bytes 196616 | tf_op jit(solution)/shard_map/ppermute | solution.py:258
  46.2 7.1 %collective-permute-start.13 = (f32[64,256]{1,0:T(8,128)S(1)}, f32[64,256]{1,0:T(8,128)S(1)}, u32[]{:S(2)}, u32[]{:S(2)}) collective-permute-start(f32[64,256]{1,0:T(8,128)S(1)} %add.61), channel_id=1, source_target_pairs={{0,32},{32,0},{1,33},{33,1},{2,34},{34,2},{3,35},{35,3},{4,36},{36... | collective-permute-start | bytes 196616 | tf_op jit(solution)/shard_map/ppermute | solution.py:202
  53.3 4.0 %collective-permute-start.14 = (f32[64,256]{1,0:T(8,128)S(1)}, f32[64,256]{1,0:T(8,128)S(1)}, u32[]{:S(2)}, u32[]{:S(2)}) collective-permute-start(f32[64,256]{1,0:T(8,128)S(1)} %add.62), channel_id=1, source_target_pairs={{0,64},{64,0},{128,192},{192,128},{1,65},{65,1},{129,193},{193,129... | collective-permute-start | bytes 196616 | tf_op jit(solution)/shard_map/ppermute | solution.py:193
  53.4 5.1 %collective-permute-start.15 = (f32[64,256]{1,0:T(8,128)S(1)}, f32[64,256]{1,0:T(8,128)S(1)}, u32[]{:S(2)}, u32[]{:S(2)}) collective-permute-start(f32[64,256]{1,0:T(8,128)S(1)} %add.62), channel_id=1, source_target_pairs={{0,128},{64,192},{128,0},{192,64},{1,129},{65,193},{129,1},{193,65... | collective-permute-start | bytes 196616 | tf_op jit(solution)/shard_map/ppermute | solution.py:193
  54.8 4.4 %collective-permute-start.16 = (f32[64,256]{1,0:T(8,128)S(1)}, f32[64,256]{1,0:T(8,128)S(1)}, u32[]{:S(2)}, u32[]{:S(2)}) collective-permute-start(f32[64,256]{1,0:T(8,128)S(1)} %add.62), channel_id=1, source_target_pairs={{0,192},{64,128},{128,64},{192,0},{1,193},{65,129},{129,65},{193,1... | collective-permute-start | bytes 196616 | tf_op jit(solution)/shard_map/ppermute | solution.py:193
  59.2 6.6 %collective-permute-start.17 = (f32[64,256]{1,0:T(8,128)S(1)}, f32[64,256]{1,0:T(8,128)S(1)}, u32[]{:S(2)}, u32[]{:S(2)}) collective-permute-start(f32[64,256]{1,0:T(8,128)S(1)} %multiply_add_fusion.1), channel_id=1, source_target_pairs={{0,16},{16,0},{1,17},{17,1},{2,18},{18,2},{3,19},{19,3},{4,20},{20... | collective-permute-start | bytes 196616 | tf_op jit(solution)/shard_map/ppermute | solution.py:208
